TPU v7x, 256 devices: a whole 4x4x8 slice. The times are simulated.
256 devices in a mesh: pipe: 32 (over y, z), tp: 8 (over x, core).
Axes of the slice: x: 4, y: 4, z: 8, core: 2. Of those that a mesh axis runs over, the one named last changes fastest.
Arguments:
- fwd_resid: bfloat16 [32, 512, 4096], P('pipe', 'tp'), may hold values from -6 to 6
- fwd_query: bfloat16 [32, 512, 4096], P('pipe', None, 'tp'), may hold values from -28 to 28
- fwd_keyval: bfloat16 [32, 2, 512, 1024], P('pipe', None, None, 'tp'), may hold values from -8 to 8
- fwd_micro: int32 [32], P('pipe'), may hold values from 0 to 3
- bwd_query: bfloat16 [32, 512, 4096], P('pipe', None, 'tp'), may hold values from -28 to 28
- bwd_keyval: bfloat16 [32, 2, 512, 1024], P('pipe', None, None, 'tp'), may hold values from -8 to 8
- grad_micro: int32 [32], P('pipe'), may hold values from 0 to 3
- grad_in: bfloat16 [32, 512, 4096], P('pipe', 'tp'), may hold values from -6 to 6
- out_weight: bfloat16 [32, 4096, 4096], P('pipe', 'tp'), may hold values from -0.09375 to 0.09375
- doc_starts: int32 [4, 4], replicated, may hold values from 0 to 511, as said below
Outputs:
- fwd_out: bfloat16 [32, 512, 4096], P('pipe', 'tp')
- grad_query: bfloat16 [32, 512, 4096], P('pipe', None, 'tp')
- grad_keyval: bfloat16 [32, 2, 512, 1024], P('pipe', None, None, 'tp')
- grad_weight: bfloat16 [32, 4096, 4096], P('pipe', 'tp')
Inputs may be any that keep to these rules, and one draw needn't show every extreme that they name: `doc_starts`: row m holds the first rows of the 4 documents of micro-batch m: it begins with 0 and rises strictly.
All inputs are finite; a program needn't handle non-finite values.
Results may differ from a plain program's by a relative error of at most 0.007.
Values may be sent and summed in bfloat16 or wider, within the bound.
A program may use at most 128 MiB of HBM per device.

v0:
```python
import math

import jax
import jax.numpy as jnp
from jax import lax
from jax.sharding import PartitionSpec as P

HD = 128


def from_behind(value, axis, steps):
    count = lax.axis_size(axis)
    pairs = [(source, (source + steps) % count) for source in range(count)]
    return lax.ppermute(value, axis, pairs)


def doc_allowed(starts, row_count):
    position = jnp.arange(row_count, dtype=jnp.int32)
    segment = jnp.sum((starts[None, :] <= position[:, None]).astype(jnp.int32), axis=1)
    causal = position[None, :] <= position[:, None]
    return causal & (segment[:, None] == segment[None, :])


def pick_starts(start_table, micro_index):
    chosen = jnp.arange(start_table.shape[0], dtype=jnp.int32) == micro_index
    return jnp.sum(jnp.where(chosen[:, None], start_table, 0), axis=0)


def head_forward(query_head, key_head, value_head, allowed):
    score_scale = 1.0 / math.sqrt(query_head.shape[-1])
    scores = jnp.dot(query_head, key_head.T, preferred_element_type=jnp.float32) * score_scale
    scores = jnp.where(allowed, scores, -1e30)
    shifted = jnp.exp(scores - jnp.max(scores, axis=1, keepdims=True))
    attn_probs = shifted / jnp.sum(shifted, axis=1, keepdims=True)
    output = jnp.dot(
        attn_probs.astype(jnp.bfloat16), value_head, preferred_element_type=jnp.float32
    ).astype(jnp.bfloat16)
    return (output, attn_probs)


def split_heads(query, keyval):
    row_count = query.shape[0]
    heads_here = query.shape[1] // HD
    groups_here = keyval.shape[2] // HD
    group_size = heads_here // groups_here
    query_heads = query.reshape(row_count, heads_here, HD).transpose(1, 0, 2)
    key_heads = jnp.repeat(
        keyval[0].reshape(row_count, groups_here, HD).transpose(1, 0, 2), group_size, axis=0
    )
    value_heads = jnp.repeat(
        keyval[1].reshape(row_count, groups_here, HD).transpose(1, 0, 2), group_size, axis=0
    )
    return (query_heads, key_heads, value_heads)


def attend(query, keyval, allowed):
    head_parts = split_heads(query, keyval)
    outputs, attn_probs = jax.vmap(head_forward, in_axes=(0, 0, 0, None))(
        head_parts[0], head_parts[1], head_parts[2], allowed
    )
    merged = outputs.transpose(1, 0, 2).reshape(query.shape[0], query.shape[1])
    return (merged, attn_probs, head_parts)


def head_backward(query_head, key_head, value_head, attn_probs, grad_head):
    score_scale = 1.0 / math.sqrt(query_head.shape[-1])
    grad_probs = jnp.dot(grad_head, value_head.T, preferred_element_type=jnp.float32)
    center = jnp.sum(attn_probs * grad_probs, axis=1, keepdims=True)
    grad_scores = (attn_probs * (grad_probs - center) * score_scale).astype(jnp.bfloat16)
    grad_query = jnp.dot(grad_scores, key_head, preferred_element_type=jnp.float32).astype(
        jnp.bfloat16
    )
    grad_key = jnp.dot(grad_scores.T, query_head, preferred_element_type=jnp.float32)
    grad_value = jnp.dot(
        attn_probs.astype(jnp.bfloat16).T, grad_head, preferred_element_type=jnp.float32
    )
    return (grad_query, grad_key, grad_value)


def attend_back(head_parts, attn_probs, grad_attn, keyval):
    query_heads, key_heads, value_heads = head_parts
    heads_here, row_count, head_dim = query_heads.shape
    groups_here = keyval.shape[2] // head_dim
    grad_heads = grad_attn.reshape(row_count, heads_here, head_dim).transpose(1, 0, 2)
    grad_query, grad_key, grad_value = jax.vmap(head_backward)(
        query_heads, key_heads, value_heads, attn_probs, grad_heads
    )
    merged_query = grad_query.transpose(1, 0, 2).reshape(row_count, heads_here * head_dim)
    key_sum = grad_key.reshape(groups_here, heads_here // groups_here, row_count, head_dim).sum(
        axis=1
    )
    value_sum = grad_value.reshape(groups_here, heads_here // groups_here, row_count, head_dim).sum(
        axis=1
    )
    stacked = (
        jnp.stack([key_sum, value_sum])
        .transpose(0, 2, 1, 3)
        .reshape(2, row_count, groups_here * head_dim)
    )
    return (merged_query, stacked.astype(jnp.bfloat16))


def shards(
    fwd_resid,
    fwd_query,
    fwd_keyval,
    fwd_micro,
    bwd_query,
    bwd_keyval,
    grad_micro,
    grad_in,
    out_weight,
    doc_starts,
):
    resid_in, query_in, keyval_in, micro_in = from_behind(
        (fwd_resid[0], fwd_query[0], fwd_keyval[0], fwd_micro), "pipe", 1
    )
    weight = out_weight[0]
    row_count = query_in.shape[0]
    allowed = doc_allowed(pick_starts(doc_starts, micro_in[0]), row_count)
    attn_out, _, _ = attend(query_in, keyval_in, allowed)
    proj_sum = lax.psum_scatter(
        jnp.dot(attn_out, weight, preferred_element_type=jnp.float32).astype(jnp.bfloat16),
        "tp",
        scatter_dimension=0,
        tiled=True,
    ).astype(jnp.float32)
    phase_out = (resid_in.astype(jnp.float32) + proj_sum).astype(jnp.bfloat16)
    whole_grad = lax.all_gather(grad_in[0], "tp", axis=0, tiled=True)
    grad_rows, micro_back = from_behind((whole_grad, grad_micro), "pipe", -1)
    allowed_back = doc_allowed(pick_starts(doc_starts, micro_back[0]), row_count)
    back_attn, attn_probs, head_parts = attend(bwd_query[0], bwd_keyval[0], allowed_back)
    grad_attn = jnp.dot(grad_rows, weight.T, preferred_element_type=jnp.float32).astype(
        jnp.bfloat16
    )
    weight_sum = jnp.dot(back_attn.T, grad_rows, preferred_element_type=jnp.float32)
    query_grad, keyval_grad = attend_back(head_parts, attn_probs, grad_attn, bwd_keyval[0])
    return (
        phase_out[None],
        query_grad[None],
        keyval_grad[None],
        weight_sum.astype(jnp.bfloat16)[None],
    )


def solution(mesh):
    return jax.shard_map(
        shards,
        mesh=mesh,
        in_specs=(
            P("pipe", "tp", None),
            P("pipe", None, "tp"),
            P("pipe", None, None, "tp"),
            P("pipe"),
            P("pipe", None, "tp"),
            P("pipe", None, None, "tp"),
            P("pipe"),
            P("pipe", "tp", None),
            P("pipe", "tp", None),
            P(),
        ),
        out_specs=(
            P("pipe", "tp", None),
            P("pipe", None, "tp"),
            P("pipe", None, None, "tp"),
            P("pipe", "tp", None),
        ),
        check_vma=False,
    )
```

profile of v0, /device:TPU:1, one launch (start us, length us, event | category | flops | bytes accessed | tf_op | source)
XLA Modules:
  0.0 184.8 jit_solution(14916090748712543174)
XLA Ops:
  7.2 0.0 all-gather.3.cloned.1.call-start
  7.2 0.7 all-gather.3.cloned.1.call-update
  7.9 0.0 reduce-scatter.2.cloned.1.call-start
  7.9 8.9 %collective-permute-start.4 = (s32[1]{0:T(128)}, s32[1]{0:T(128)}, u32[]{:S(2)}, u32[]{:S(2)}) collective-permute-start(s32[1]{0:T(128)} %param.16), channel_id=1, source_target_pairs={{0,248},{8,0},{16,8},{24,16},{32,24},{40,32},{48,40},{56,48},{64,5... | collective-permute-start | bytes 20 | tf_op jit(solution)/shard_map/ppermute | solution.py:14
  16.9 1.3 copy.38
  18.1 0.1 collective-permute-start.2
  18.2 0.6 iota_compare_fusion.3
  18.9 4.0 %collective-permute-done.1 = s32[1]{0:T(128)} collective-permute-done((s32[1]{0:T(128)}, s32[1]{0:T(128)}, u32[]{:S(2)}, u32[]{:S(2)}) %collective-permute-start.1) | collective-permute-done | bytes 36 | tf_op jit(solution)/shard_map/ppermute | solution.py:14
  22.8 0.6 iota_compare_fusion.4
  23.5 0.8 select_reduce_fusion
  24.2 0.1 convert_reduce_fusion.1
  24.3 0.2 fusion.48
  24.5 2.8 %collective-permute-done.3 = bf16[2,512,128]{2,1,0:T(8,128)(2,1)S(1)} collective-permute-done((bf16[2,512,128]{2,1,0:T(8,128)(2,1)}, bf16[2,512,128]{2,1,0:T(8,128)(2,1)S(1)}, u32[]{:S(2)}, u32[]{:S(2)}) %collective-permute-start.3) | collective-permute-done | bytes 262176 | tf_op jit(solution)/shard_map/ppermute | solution.py:14
  27.4 0.1 copy.40
  27.5 11.1 %collective-permute-done.2 = bf16[512,512]{0,1:T(8,128)(2,1)S(1)} collective-permute-done((bf16[512,512]{0,1:T(8,128)(2,1)S(1)}, bf16[512,512]{0,1:T(8,128)(2,1)S(1)}, u32[]{:S(2)}, u32[]{:S(2)}) %collective-permute-start.2) | collective-permute-done | bytes 524320 | tf_op jit(solution)/shard_map/ppermute | solution.py:14
  38.6 0.3 copy.39
  38.9 0.7 fusion.56
  39.6 2.1 %fusion.74 = (f32[4,512]{1,0:T(4,128)S(1)}, f32[4,512,512]{1,2,0:T(8,128)S(1)}) fusion(f32[4,512,512]{1,2,0:T(8,128)S(1)} %fusion.56, pred[512,512]{0,1:T(8,128)(4,1)S(1)} %fusion.48), kind=kOutput, calls=%fused_computation.85 | output fusion | flops 6291967 | bytes 8658944 | tf_op jit(solution)/shard_map/vmap()/sub | solution.py:33
  41.7 0.0 copy-start
  41.7 0.5 fusion.30
  42.2 1.8 copy-done
  44.0 4.4 %convolution_convert_fusion.1 = bf16[512,4096]{1,0:T(8,128)(2,1)} fusion(bf16[512,512]{0,1:T(8,128)(2,1)S(1)} %bitcast.71, bf16[1,512,4096]{2,1,0:T(8,128)(2,1)S(1)} %copy-done), kind=kOutput, calls=%fused_computation.4 | convolution fusion | flops 2149580800 | bytes 8912896 | tf_op jit(solution)/shard_map/dot_general | solution.py:123
  48.4 0.0 reduce-scatter.2.cloned.1.call-update
  48.4 0.2 all-gather.3.cloned.1.call-done
  48.6 5.2 %collective-permute-start.5 = (bf16[512,4096]{1,0:T(8,128)(2,1)}, bf16[512,4096]{1,0:T(8,128)(2,1)}, u32[]{:S(2)}, u32[]{:S(2)}) collective-permute-start(bf16[512,4096]{1,0:T(8,128)(2,1)} %bitcast.76), channel_id=1, source_target_pairs={{0,248},{8,0},{16,8},{24,16},{32,24},{40,32},{48,40},{56,48},{64,5... | collective-permute-start | bytes 12582920 | tf_op jit(solution)/shard_map/ppermute | solution.py:14
  53.9 0.1 copy.43
  54.0 0.1 reshape_squeeze.3
  54.1 0.1 copy.46
  54.3 0.8 fusion.54
  55.0 0.1 convert_reduce_fusion
  55.1 0.2 fusion.47
  55.3 2.1 %fusion.75 = (f32[4,512]{1,0:T(4,128)S(1)}, f32[4,512,512]{1,2,0:T(8,128)S(1)}) fusion(f32[4,512,512]{1,2,0:T(8,128)S(1)} %fusion.54, pred[512,512]{0,1:T(8,128)(4,1)S(1)} %fusion.47), kind=kOutput, calls=%fused_computation.86 | output fusion | flops 6291967 | bytes 8658944 | tf_op jit(solution)/shard_map/vmap()/sub | solution.py:33
  57.5 0.5 convolution_convert_fusion.2
  57.9 1.5 copy-done.4
  59.4 10.7 %collective-permute-done = bf16[64,4096]{1,0:T(8,128)(2,1)S(1)} collective-permute-done((bf16[64,4096]{1,0:T(8,128)(2,1)S(1)}, bf16[64,4096]{1,0:T(8,128)(2,1)S(1)}, u32[]{:S(2)}, u32[]{:S(2)}) %collective-permute-start) | collective-permute-done | bytes 524320 | tf_op jit(solution)/shard_map/ppermute | solution.py:14
  70.1 19.4 %reduce-scatter.2.cloned.1.call-done = bf16[64,4096]{1,0:T(8,128)(2,1)} async-done(((bf16[512,4096]{1,0:T(8,128)(2,1)}), bf16[64,4096]{1,0:T(8,128)(2,1)}) %reduce-scatter.2.cloned.1.call-update) | async-done | bytes 524304 | tf_op jit(solution)/shard_map/reduce_scatter | solution.py:122
  89.5 2.0 %fusion.49 = bf16[1,64,4096]{2,1,0:T(8,128)(2,1)} fusion(bf16[64,4096]{1,0:T(8,128)(2,1)} %reduce-scatter.2.cloned.1.call-done, bf16[64,4096]{1,0:T(8,128)(2,1)S(1)} %collective-permute-done), kind=kLoop, calls=%fused_computation.47 | loop fusion | flops 1048576 | bytes 1572864 | tf_op jit(solution)/shard_map/broadcast_in_dim | solution.py:139
  91.5 52.3 %collective-permute-done.5 = bf16[512,4096]{1,0:T(8,128)(2,1)} collective-permute-done((bf16[512,4096]{1,0:T(8,128)(2,1)}, bf16[512,4096]{1,0:T(8,128)(2,1)}, u32[]{:S(2)}, u32[]{:S(2)}) %collective-permute-start.5) | collective-permute-done | bytes 4194336 | tf_op jit(solution)/shard_map/ppermute | solution.py:14
  143.8 5.8 %fusion.27 = bf16[512,512]{0,1:T(8,128)(2,1)S(1)} fusion(bf16[512,4096]{1,0:T(8,128)(2,1)} %collective-permute-done.5, bf16[1,512,4096]{2,1,0:T(8,128)(2,1)} %param.18), kind=kOutput, calls=%fused_computation.31 | convolution fusion | flops 2147745792 | bytes 8912896 | tf_op jit(solution)/shard_map/dot_general | solution.py:133
  149.6 0.3 copy.45
  149.9 2.8 %fusion.51 = f32[4,512,512]{1,2,0:T(8,128)} fusion(bf16[512,4,128]{2,0,1:T(8,128)(2,1)S(1)} %copy.45, bf16[512,128]{0,1:T(8,128)(2,1)S(1)} %copy.46), kind=kOutput, calls=%fused_computation.49 | convolution fusion | flops 268435456 | bytes 4849664 | tf_op jit(solution)/shard_map/vmap()/dot_general | solution.py:67
  152.7 0.6 copy-done.5
  153.3 0.7 fusion.41
  154.1 7.8 %fusion.42 = bf16[1,1,512,128]{3,2,1,0:T(8,128)(2,1)S(1)} fusion(f32[4,512,512]{1,2,0:T(8,128)} %fusion.51, bf16[512,4,128]{2,1,0:T(4,128)(2,1)S(1)} %reshape_squeeze.3, f32[4,512,512]{1,2,0:T(8,128)} %copy-done.4, f32[4,512]{1,0:T(4,128)S(1)} %get-tuple-element.24), kind=kOutput, calls=%fused_computation.40 | convolution fusion | flops 275843584 | bytes 9052160 | tf_op jit(solution)/shard_map/vmap()/dot_general | solution.py:73
  161.8 7.8 %fusion.31 = bf16[4,512,128]{1,2,0:T(8,128)(2,1)S(1)} fusion(f32[4,512,512]{1,2,0:T(8,128)} %fusion.51, bf16[512,128]{0,1:T(8,128)(2,1)S(1)} %copy.43, f32[4,512,512]{1,2,0:T(8,128)} %copy-done.4, f32[4,512]{1,0:T(4,128)S(1)} %get-tuple-element.24), kind=kOutput, calls=%fused_computation.34 | convolution fusion | flops 276040192 | bytes 9052160 | tf_op jit(solution)/shard_map/vmap()/dot_general | solution.py:70
  169.6 1.0 copy.50
  170.7 0.7 maximum_bitcast_fusion
  171.4 6.6 %fusion.3 = bf16[1,512,4096]{2,1,0:T(8,128)(2,1)} fusion(bf16[512,512]{0,1:T(8,128)(2,1)S(1)} %bitcast.79, bf16[512,4096]{1,0:T(8,128)(2,1)} %collective-permute-done.5), kind=kOutput, calls=%fused_computation.5 | convolution fusion | flops 2149580800 | bytes 8912896 | tf_op jit(solution)/shard_map/dot_general | solution.py:136
  (14 shorter events, 0.1 us)
Async XLA Ops:
  7.2 41.5 %all-gather.3.cloned.1.call-start = ((), (), s32[]{:S(2)}) async-start(), calls=%async_computation.2 | async-start | bytes 4718592 | tf_op jit(solution)/shard_map/all_gather | solution.py:129
  7.9 81.6 %reduce-scatter.2.cloned.1.call-start = ((), (), s32[]{:S(2)}) async-start(), calls=%async_computation.1 | async-start | bytes 4718592 | tf_op jit(solution)/shard_map/reduce_scatter | solution.py:122
  7.9 10.3 %collective-permute-start.4 = (s32[1]{0:T(128)}, s32[1]{0:T(128)}, u32[]{:S(2)}, u32[]{:S(2)}) collective-permute-start(s32[1]{0:T(128)} %param.16), channel_id=1, source_target_pairs={{0,248},{8,0},{16,8},{24,16},{32,24},{40,32},{48,40},{56,48},{64,5... | collective-permute-start | bytes 20 | tf_op jit(solution)/shard_map/ppermute | solution.py:14
  16.9 6.0 %collective-permute-start.1 = (s32[1]{0:T(128)}, s32[1]{0:T(128)}, u32[]{:S(2)}, u32[]{:S(2)}) collective-permute-start(s32[1]{0:T(128)} %param.13), channel_id=1, source_target_pairs={{0,8},{8,16},{16,24},{24,32},{32,40},{40,48},{48,56},{56,64},{64,7... | collective-permute-start | bytes 20 | tf_op jit(solution)/shard_map/ppermute | solution.py:14
  16.9 10.5 %collective-permute-start.3 = (bf16[2,512,128]{2,1,0:T(8,128)(2,1)}, bf16[2,512,128]{2,1,0:T(8,128)(2,1)S(1)}, u32[]{:S(2)}, u32[]{:S(2)}) collective-permute-start(bf16[2,512,128]{2,1,0:T(8,128)(2,1)} %bitcast.78), channel_id=1, source_target_pairs={{0,8},{8,16},{16,24},{24,32},{32,40},{40,48},{48,56},{56,64},{64,7... | collective-permute-start | bytes 786440 | tf_op jit(solution)/shard_map/ppermute | solution.py:14
  18.1 20.4 %collective-permute-start.2 = (bf16[512,512]{0,1:T(8,128)(2,1)S(1)}, bf16[512,512]{0,1:T(8,128)(2,1)S(1)}, u32[]{:S(2)}, u32[]{:S(2)}) collective-permute-start(bf16[512,512]{0,1:T(8,128)(2,1)S(1)} %bitcast.73), channel_id=1, source_target_pairs={{0,8},{8,16},{16,24},{24,32},{32,40},{40,48},{48,56},{56,64},{64,7... | collective-permute-start | bytes 1572872 | tf_op jit(solution)/shard_map/ppermute | solution.py:14
  41.7 2.2 %copy-start = (bf16[1,512,4096]{2,1,0:T(8,128)(2,1)S(1)}, bf16[1,512,4096]{2,1,0:T(8,128)(2,1)}, u32[]{:S(2)}) copy-start(bf16[1,512,4096]{2,1,0:T(8,128)(2,1)} %param.18) | copy-start | bytes 12582916
  48.4 5.5 %copy-start.3 = (bf16[1,64,4096]{2,1,0:T(8,128)(2,1)S(1)}, bf16[1,64,4096]{2,1,0:T(8,128)(2,1)}, u32[]{:S(2)}) copy-start(bf16[1,64,4096]{2,1,0:T(8,128)(2,1)} %param.10) | copy-start | bytes 1572868
  48.4 5.5 %copy-start.2 = (bf16[1,2,512,128]{3,2,1,0:T(8,128)(2,1)S(1)}, bf16[1,2,512,128]{3,2,1,0:T(8,128)(2,1)}, u32[]{:S(2)}) copy-start(bf16[1,2,512,128]{3,2,1,0:T(8,128)(2,1)} %param.15) | copy-start | bytes 786436
  48.4 5.6 %copy-start.1 = (bf16[1,512,512]{2,1,0:T(8,128)(2,1)S(1)}, bf16[1,512,512]{2,1,0:T(8,128)(2,1)}, u32[]{:S(2)}) copy-start(bf16[1,512,512]{2,1,0:T(8,128)(2,1)} %param.14) | copy-start | bytes 1572868
  48.6 95.2 %collective-permute-start.5 = (bf16[512,4096]{1,0:T(8,128)(2,1)}, bf16[512,4096]{1,0:T(8,128)(2,1)}, u32[]{:S(2)}, u32[]{:S(2)}) collective-permute-start(bf16[512,4096]{1,0:T(8,128)(2,1)} %bitcast.76), channel_id=1, source_target_pairs={{0,248},{8,0},{16,8},{24,16},{32,24},{40,32},{48,40},{56,48},{64,5... | collective-permute-start | bytes 12582920 | tf_op jit(solution)/shard_map/ppermute | solution.py:14
  53.8 16.2 %collective-permute-start = (bf16[64,4096]{1,0:T(8,128)(2,1)S(1)}, bf16[64,4096]{1,0:T(8,128)(2,1)S(1)}, u32[]{:S(2)}, u32[]{:S(2)}) collective-permute-start(bf16[64,4096]{1,0:T(8,128)(2,1)S(1)} %bitcast.77), channel_id=1, source_target_pairs={{0,8},{8,16},{16,24},{24,32},{32,40},{40,48},{48,56},{56,64},{64,7... | collective-permute-start | bytes 1572872 | tf_op jit(solution)/shard_map/ppermute | solution.py:14
  57.5 2.0 %copy-start.4 = (f32[4,512,512]{1,2,0:T(8,128)}, f32[4,512,512]{1,2,0:T(8,128)S(1)}, u32[]{:S(2)}) copy-start(f32[4,512,512]{1,2,0:T(8,128)S(1)} %get-tuple-element.25) | copy-start | bytes 12582916
  149.9 3.4 %copy-start.5 = (f32[4,512,512]{1,2,0:T(8,128)S(1)}, f32[4,512,512]{1,2,0:T(8,128)}, u32[]{:S(2)}) copy-start(f32[4,512,512]{1,2,0:T(8,128)} %copy-done.4) | copy-start | bytes 12582916
Sparse Core Ops, SparseCore 0:
  9.8 38.7 all-gather.2
  51.8 37.7 reduce-scatter.1
where the time goes:
time: 185 us
  waiting for transfers between devices  101 us (55%)
  matrix products  38.3 us (21%)
  starting transfers between devices  14.3 us (8%)
  between operations  14.3 us (8%)
  other arithmetic  9.55 us (5%)
  local copies, waits for them, and re-layouts  7.24 us (4%)
    ppermute x6, waiting for transfers between devices, from_behind(): return lax.ppermute(value, axis, pairs)  80.9 us
    reduce_scatter x1, waiting for transfers between devices, shards(): lax.psum_scatter(jnp.dot(attn_out, weight, preferred_element_type=jnp.flo...  19.4 us
    ppermute x6, starting transfers between devices, from_behind(): return lax.ppermute(value, axis, pairs)  14.2 us
    dot_general x1, matrix products, head_backward(): jnp.dot(grad_scores, key_head, preferred_element_type=jnp.float32)  7.79 us
    dot_general x1, matrix products, head_backward(): jnp.dot(grad_scores.T, query_head, preferred_element_type=jnp.float32)  7.77 us
    dot_general x1, matrix products, shards(): jnp.dot(back_attn.T, grad_rows, preferred_element_type=jnp.float32)  6.61 us
    unnamed x14, local copies, waits for them, and re-layouts  6.16 us
    dot_general x1, matrix products, shards(): jnp.dot(grad_rows, weight.T, preferred_element_type=jnp.float32)  5.82 us
  transfers between devices with their start and end apart: 8, of which 7 were waited for; matrix products, arithmetic and copies ran while one was open for 10% of the time, Pallas kernels for 0%

commit v1 on v0

v1 whole, which is shorter than its diff:
```python
import functools
import math

import jax
import jax.numpy as jnp
from jax import lax
from jax.experimental import pallas as pl
from jax.experimental.pallas import tpu as pltpu
from jax.sharding import PartitionSpec as P

MESH = pl.DeviceIdType.MESH
F32 = jnp.float32
BF16 = jnp.bfloat16
R = 512
D = 4096
HD = 128
HALF = D // 2
SCALE = 1.0 / math.sqrt(HD)
EXP_SCALE = SCALE * math.log2(math.e)
MASKED = -1e30
CHUNKS = 4
CROWS = 64 // CHUNKS
TILE = 512
OPP, LEFT, RIGHT, OWN = 0, 1, 2, 3


def dot(a, b):
    return jnp.dot(a, b, preferred_element_type=F32)


def dot_nt(a, b):
    return lax.dot_general(a, b, (((1,), (1,)), ((), ())), preferred_element_type=F32)


def kernel(
    fwd_micro, grad_micro, starts, resid, fq, fkv, bq, bkv, grad, weight,
    out, gq, gkv, gw,
    fq_v, fkv_v, bq_v, bkv_v, w_v, g_v, attn_out, attn_in, resid_in, mic_out, mic_in,
    bias_f, bias_b, kt_v, vt_v, pt_v, bat_v, acc_v, ga_v, dk_v, dv_v, gq_v, gkv_v, gw_v,
    part, recvp, opp_sum, side_sum, rel_l, rel_r, fin_l, fin_r, acc_r, acc_l, out_v,
    ld_sem, st_sem, gw_sem,
    z_s, z_r, mic_s, mic_r, at_s, at_r, rs_s, rs_r,
    xr_s, xl_s, fl_r, fr_r, yr_s, yl_s, fl2_r, fr2_r, p_s, p_r,
    pp_s, pp_r, sr_s, sl_s, sl_r, sr_r,
):
    pipe, tp = lax.axis_index("pipe"), lax.axis_index("tp")
    n_pipe = lax.axis_size("pipe")
    core = lax.rem(tp, 2)
    partner = tp + 1 - 2 * core
    right, left, opp = lax.rem(tp + 2, 8), lax.rem(tp + 6, 8), lax.rem(tp + 4, 8)
    chip = lax.div(tp, 2)
    nxt, prv = lax.rem(pipe + 1, n_pipe), lax.rem(pipe + n_pipe - 1, n_pipe)

    def rcopy(src, dst, send, recv, device):
        return pltpu.make_async_remote_copy(
            src_ref=src, dst_ref=dst, send_sem=send, recv_sem=recv, device_id=device, device_id_type=MESH
        )

    def landed(dst, recv):
        pltpu.make_async_copy(dst, dst, recv).wait()

    loads = [
        pltpu.make_async_copy(src, dst, ld_sem.at[i])
        for i, (src, dst) in enumerate(
            [(fkv, fkv_v), (fq, fq_v), (bkv, bkv_v), (bq, bq_v), (weight, w_v)]
        )
    ]
    for load in loads:
        load.start()
    mic_out[...] = jnp.full(mic_out.shape, grad_micro[0], jnp.int32)

    barrier = pltpu.get_barrier_semaphore()
    peers = ((pipe, partner), (pipe, right), (pipe, left), (nxt, tp), (prv, tp))
    for peer in peers:
        pl.semaphore_signal(barrier, inc=1, device_id=peer, device_id_type=MESH)

    first = [starts[0, d] for d in range(4)]
    for m in range(1, 4):
        first = [jnp.where(fwd_micro[0] == m, starts[m, d], first[d]) for d in range(4)]

    @pl.loop(0, 4)
    def _(block):
        row0 = pl.multiple_of(block * 128, 128)
        row = lax.broadcasted_iota(jnp.int32, (128, R), 0) + row0
        column = lax.broadcasted_iota(jnp.int32, (128, R), 1)
        begin = jnp.zeros((128, R), jnp.int32)
        for d in range(4):
            begin = jnp.maximum(begin, jnp.where(row >= first[d], first[d], 0))
        bias_f[pl.ds(row0, 128), :] = jnp.where((column >= begin) & (column <= row), 0.0, MASKED)

    pl.semaphore_wait(barrier, len(peers))

    def rows_of(shard, k):
        return pl.ds(pl.multiple_of(shard * 64 + k * CROWS, CROWS), CROWS)

    def z_copy(k):
        return rcopy(
            grad.at[pl.ds(pl.multiple_of(k * CROWS, CROWS), CROWS), :], g_v.at[rows_of(tp, k), :],
            z_s.at[k], z_r.at[k], (prv, tp),
        )

    mic = rcopy(mic_out, mic_in, mic_s, mic_r, (prv, tp))
    mic.start()
    for k in range(CHUNKS):
        z_copy(k).start()

    loads[0].wait()
    loads[1].wait()

    def attn_copy(h):
        return rcopy(attn_out.at[h], attn_in.at[h], at_s.at[h], at_r.at[h], (nxt, tp))

    @pl.loop(0, 4)
    def _(h):
        cols = pl.ds(pl.multiple_of(h * HD, HD), HD)
        for b in range(2):
            n = 256 * (b + 1)
            rows = slice(256 * b, n)
            scores = dot_nt(fq_v[rows, cols], fkv_v[0, :n, :]) + bias_f[rows, :n]
            shifted = jnp.exp2((scores - jnp.max(scores, axis=1, keepdims=True)) * EXP_SCALE)
            total = jnp.sum(shifted, axis=1, keepdims=True)
            attn_out[h, rows, :] = (dot(shifted.astype(BF16), fkv_v[1, :n, :]) * (1.0 / total)).astype(BF16)
        attn_copy(h).start()

    resid_copy = rcopy(resid, resid_in, rs_s, rs_r, (nxt, tp))
    resid_copy.start()

    loads[2].wait()
    loads[3].wait()
    mic.wait_recv()
    micro = mic_in[0:1, :]
    begins = []
    for d in range(4):
        value = jnp.zeros((1, 128), jnp.int32)
        for m in range(4):
            value = value + jnp.where(micro == m, starts[m, d], 0)
        begins.append(value)

    @pl.loop(0, 4)
    def _(block):
        col0 = pl.multiple_of(block * 128, 128)
        query = lax.broadcasted_iota(jnp.int32, (1, 128), 1) + col0
        begin = jnp.zeros((1, 128), jnp.int32)
        for d in range(4):
            begin = jnp.maximum(begin, jnp.where(query >= begins[d], begins[d], 0))
        key = lax.broadcasted_iota(jnp.int32, (R, 128), 0)
        bias_b[:, pl.ds(col0, 128)] = jnp.where((key >= begin) & (key <= query), 0.0, MASKED)

    kt_v[...] = bkv_v[0].astype(F32).T.astype(BF16)
    vt_v[...] = bkv_v[1].astype(F32).T.astype(BF16)
    dk_v[...] = jnp.zeros_like(dk_v)
    dv_v[...] = jnp.zeros_like(dv_v)

    half_a, half_b = pl.ds(0, HALF), pl.ds(HALF, HALF)

    def x_copies(k):
        mine = g_v.at[rows_of(tp, k), :]
        return (
            rcopy(mine, mine, xr_s.at[k], fl_r.at[k], (pipe, right)),
            rcopy(mine, mine, xl_s.at[k], fr_r.at[k], (pipe, left)),
            rcopy(mine, mine, p_s.at[0, k], p_r.at[0, k], (pipe, partner)),
        )

    def left_copies(k):
        theirs = g_v.at[rows_of(left, k), half_a]
        whole = g_v.at[rows_of(left, k), :]
        return (
            rcopy(theirs, theirs, yr_s.at[k], fl2_r.at[k], (pipe, right)),
            rcopy(whole, whole, p_s.at[1, k], p_r.at[1, k], (pipe, partner)),
        )

    def right_copies(k):
        theirs = g_v.at[rows_of(right, k), half_b]
        whole = g_v.at[rows_of(right, k), :]
        return (
            rcopy(theirs, theirs, yl_s.at[k], fr2_r.at[k], (pipe, left)),
            rcopy(whole, whole, p_s.at[2, k], p_r.at[2, k], (pipe, partner)),
        )

    def opp_copy(k):
        whole = g_v.at[rows_of(opp, k), :]
        return rcopy(whole, whole, p_s.at[3, k], p_r.at[3, k], (pipe, partner))

    def from_next(k):
        landed(g_v.at[rows_of(tp, k), :], z_r.at[k])
        for copy in x_copies(k):
            copy.start()

    def from_sides(k):
        landed(g_v.at[rows_of(left, k), :], fl_r.at[k])
        for copy in left_copies(k):
            copy.start()
        landed(g_v.at[rows_of(right, k), :], fr_r.at[k])
        for copy in right_copies(k):
            copy.start()

    def from_opp(k):
        landed(g_v.at[rows_of(opp, k), half_a], fl2_r.at[k])
        landed(g_v.at[rows_of(opp, k), half_b], fr2_r.at[k])
        opp_copy(k).start()

    @pl.loop(0, 4)
    def _(k):
        from_next(k)
        cols = pl.ds(pl.multiple_of(k * HD, HD), HD)
        for b in range(2):
            n = 256 * (b + 1)
            rows = slice(256 * b, n)
            scores = dot_nt(bkv_v[0, :n, :], bq_v[rows, cols]) + bias_b[:n, rows]
            shifted = jnp.exp2((scores - jnp.max(scores, axis=0, keepdims=True)) * EXP_SCALE)
            total = jnp.sum(shifted, axis=0, keepdims=True)
            probs = (shifted * (1.0 / total)).astype(BF16)
            pt_v[k, :n, rows] = probs
            bat_v[cols, rows] = dot(vt_v[:, :n], probs).astype(BF16)

        @pl.when(k >= 1)
        def _():
            from_sides(k - 1)

        @pl.when(k >= 2)
        def _():
            from_opp(k - 2)

    loads[4].wait()
    for h in range(4):
        landed(attn_in.at[h], at_r.at[h])
    chip_of = (lax.rem(chip + 2, 4), lax.rem(chip + 3, 4), lax.rem(chip + 1, 4), chip)

    def project(pair, tiles):
        def block(slot):
            rows = pl.ds(pl.multiple_of(chip_of[slot] * 128, 128), 128)
            return jnp.concatenate([attn_in[h, rows, :] for h in range(4)], axis=1)

        lhs = jnp.concatenate([block(slot) for slot in pair], axis=0)

        @pl.loop(tiles[0], tiles[1])
        def _(tile):
            cols = pl.ds(pl.multiple_of(tile * TILE, TILE), TILE)
            product = dot(lhs, w_v[:, cols]).astype(BF16)
            for i, slot in enumerate(pair):
                for c in range(2):
                    part[slot, c, :, cols] = product[128 * i + 64 * c : 128 * i + 64 * c + 64, :]

    halves = (half_a, half_b)

    def pp_copy(slot, half):
        return rcopy(
            part.at[slot, 1 - core, :, halves[half]], recvp.at[slot, :, halves[half]],
            pp_s.at[slot, half], pp_r.at[slot, half], (pipe, partner),
        )

    def chip_sum(slot, half, cols):
        begin = half * HALF + cols
        window = pl.ds(pl.multiple_of(begin, TILE), TILE)
        return part[slot, core, :, window].astype(F32) + recvp[slot, :, window].astype(F32)

    for pair in ((OPP, LEFT), (RIGHT, OWN)):
        for half in range(2):
            project(pair, (4 * half, 4 * half + 4))
            for slot in pair:
                pp_copy(slot, half).start()

    def opp_half(half):
        landed(recvp.at[OPP, :, halves[half]], pp_r.at[OPP, half])

        @pl.loop(0, HALF, step=TILE)
        def _(cols):
            opp_sum[half, :, pl.ds(pl.multiple_of(cols, TILE), TILE)] = chip_sum(OPP, half, cols).astype(BF16)

    send_opp_r = rcopy(opp_sum.at[0], rel_l, sr_s.at[0], sl_r.at[0], (pipe, right))
    send_opp_l = rcopy(opp_sum.at[1], rel_r, sl_s.at[0], sr_r.at[0], (pipe, left))
    send_side_l = rcopy(side_sum.at[0], fin_r.at[0], sl_s.at[1], sr_r.at[1], (pipe, left))
    send_side_r = rcopy(side_sum.at[1], fin_l.at[1], sr_s.at[1], sl_r.at[1], (pipe, right))
    send_acc_r = rcopy(acc_r, fin_l.at[0], sr_s.at[2], sl_r.at[2], (pipe, right))
    send_acc_l = rcopy(acc_l, fin_r.at[1], sl_s.at[2], sr_r.at[2], (pipe, left))

    opp_half(0)
    from_sides(3)
    send_opp_r.start()
    opp_half(1)
    from_opp(2)
    send_opp_l.start()

    def side_half(slot, half):
        landed(recvp.at[slot, :, halves[half]], pp_r.at[slot, half])

        @pl.loop(0, HALF, step=TILE)
        def _(cols):
            side_sum[half, :, pl.ds(pl.multiple_of(cols, TILE), TILE)] = chip_sum(slot, half, cols).astype(BF16)

    side_half(LEFT, 0)
    side_half(RIGHT, 1)
    from_opp(3)
    send_side_l.start()
    send_side_r.start()

    for kind, shard in enumerate((tp + 1 - 2 * core, left + 1 - 2 * core, right + 1 - 2 * core, opp + 1 - 2 * core)):
        for k in range(CHUNKS):
            landed(g_v.at[rows_of(shard, k), :], p_r.at[kind, k])

    acc_v[...] = jnp.zeros_like(acc_v)

    @pl.loop(0, D // TILE)
    def _(tile):
        cols = pl.ds(pl.multiple_of(tile * TILE, TILE), TILE)
        acc_v[...] += dot_nt(g_v[:, cols], w_v[:, cols])

    ga_v[...] = acc_v[...].astype(BF16)

    def gw_copy(tile):
        cols = pl.ds(pl.multiple_of(tile * TILE, TILE), TILE)
        return pltpu.make_async_copy(gw_v.at[:, cols], gw.at[:, cols], gw_sem.at[tile])

    @pl.loop(0, D // TILE)
    def _(tile):
        cols = pl.ds(pl.multiple_of(tile * TILE, TILE), TILE)
        gw_v[:, cols] = dot(bat_v[...], g_v[:, cols]).astype(BF16)
        gw_copy(tile).start()

    landed(rel_l, sl_r.at[0])
    landed(recvp.at[RIGHT, :, half_a], pp_r.at[RIGHT, 0])
    landed(rel_r, sr_r.at[0])
    landed(recvp.at[LEFT, :, half_b], pp_r.at[LEFT, 1])

    @pl.loop(0, HALF, step=TILE)
    def _(cols):
        window = pl.ds(pl.multiple_of(cols, TILE), TILE)
        acc_r[:, window] = (chip_sum(RIGHT, 0, cols) + rel_l[:, window].astype(F32)).astype(BF16)
        acc_l[:, window] = (chip_sum(LEFT, 1, cols) + rel_r[:, window].astype(F32)).astype(BF16)

    send_acc_r.start()
    send_acc_l.start()

    @pl.loop(0, 4)
    def _(h):
        cols = pl.ds(pl.multiple_of(h * HD, HD), HD)
        for b in range(2):
            n = 256 * (b + 1)
            rows = slice(256 * b, n)
            grad_rows = ga_v[rows, cols]
            dprob = dot_nt(bkv_v[1, :n, :], grad_rows)
            probs = pt_v[h, :n, rows]
            wide = probs.astype(F32)
            delta = jnp.sum(wide * dprob, axis=0, keepdims=True)
            dscore = (wide * (dprob - delta) * SCALE).astype(BF16)
            gq_v[rows, cols] = dot(kt_v[:, :n], dscore).T.astype(BF16)
            dk_v[:n, :] += dot(dscore, bq_v[rows, cols])
            dv_v[:n, :] += dot(probs, grad_rows)

    gkv_v[0] = dk_v[...].astype(BF16)
    gkv_v[1] = dv_v[...].astype(BF16)
    stores = [pltpu.make_async_copy(gq_v, gq, st_sem.at[0]), pltpu.make_async_copy(gkv_v, gkv, st_sem.at[1])]
    for store in stores:
        store.start()

    resid_copy.wait_recv()
    for half in range(2):
        landed(recvp.at[OWN, :, halves[half]], pp_r.at[OWN, half])
        landed(fin_l.at[half], sl_r.at[2 if half == 0 else 1])
        landed(fin_r.at[half], sr_r.at[1 if half == 0 else 2])

        @pl.loop(0, HALF, step=TILE)
        def _(cols):
            window = pl.ds(pl.multiple_of(cols, TILE), TILE)
            place = pl.ds(pl.multiple_of(half * HALF + cols, TILE), TILE)
            total = chip_sum(OWN, half, cols) + fin_l[half, :, window].astype(F32) + fin_r[half, :, window].astype(F32)
            out_v[:, place] = (resid_in[:, place].astype(F32) + total).astype(BF16)

        store = pltpu.make_async_copy(out_v.at[:, halves[half]], out.at[:, halves[half]], st_sem.at[2 + half])
        store.start()
        stores.append(store)

    mic.wait_send()
    resid_copy.wait_send()
    for h in range(4):
        attn_copy(h).wait_send()
    for k in range(CHUNKS):
        z_copy(k).wait_send()
        for copy in (*x_copies(k), *left_copies(k), *right_copies(k), opp_copy(k)):
            copy.wait_send()
    for slot in range(4):
        for half in range(2):
            pp_copy(slot, half).wait_send()
    for copy in (send_opp_r, send_opp_l, send_side_l, send_side_r, send_acc_r, send_acc_l):
        copy.wait_send()
    for tile in range(D // TILE):
        gw_copy(tile).wait()
    for store in stores:
        store.wait()


def shards(fwd_resid, fwd_query, fwd_keyval, fwd_micro, bwd_query, bwd_keyval, grad_micro, grad_in, out_weight, doc_starts):
    any_space = pl.BlockSpec(memory_space=pl.ANY)
    smem = pl.BlockSpec(memory_space=pltpu.SMEM)
    dma = pltpu.SemaphoreType.DMA
    vmem = pltpu.VMEM
    scratch = [
        vmem((R, R), BF16), vmem((2, R, HD), BF16), vmem((R, R), BF16), vmem((2, R, HD), BF16),
        vmem((R, D), BF16), vmem((R, D), BF16),
        vmem((4, R, HD), BF16), vmem((4, R, HD), BF16), vmem((64, D), BF16),
        vmem((8, 128), jnp.int32), vmem((8, 128), jnp.int32),
        vmem((R, R), F32), vmem((R, R), F32), vmem((HD, R), BF16), vmem((HD, R), BF16),
        vmem((4, R, R), BF16), vmem((R, R), BF16), vmem((R, R), F32), vmem((R, R), BF16),
        vmem((R, HD), F32), vmem((R, HD), F32), vmem((R, R), BF16), vmem((2, R, HD), BF16), vmem((R, D), BF16),
        vmem((4, 2, 64, D), BF16), vmem((4, 64, D), BF16), vmem((2, 64, HALF), BF16), vmem((2, 64, HALF), BF16),
        vmem((64, HALF), BF16), vmem((64, HALF), BF16), vmem((2, 64, HALF), BF16), vmem((2, 64, HALF), BF16),
        vmem((64, HALF), BF16), vmem((64, HALF), BF16), vmem((64, D), BF16),
        dma((5,)), dma((4,)), dma((D // TILE,)),
        dma((CHUNKS,)), dma((CHUNKS,)), dma, dma, dma((4,)), dma((4,)), dma, dma,
        dma((CHUNKS,)), dma((CHUNKS,)), dma((CHUNKS,)), dma((CHUNKS,)),
        dma((CHUNKS,)), dma((CHUNKS,)), dma((CHUNKS,)), dma((CHUNKS,)),
        dma((4, CHUNKS)), dma((4, CHUNKS)),
        dma((4, 2)), dma((4, 2)), dma((3,)), dma((3,)), dma((3,)), dma((3,)),
    ]
    out, gq, gkv, gw = pl.pallas_call(
        kernel,
        out_shape=(
            jax.ShapeDtypeStruct((64, D), BF16),
            jax.ShapeDtypeStruct((R, R), BF16),
            jax.ShapeDtypeStruct((2, R, HD), BF16),
            jax.ShapeDtypeStruct((R, D), BF16),
        ),
        in_specs=[smem] * 3 + [any_space] * 7,
        out_specs=(any_space,) * 4,
        scratch_shapes=scratch,
        compiler_params=pltpu.CompilerParams(
            collective_id=0, has_side_effects=True, vmem_limit_bytes=60 * 1024 * 1024
        ),
    )(
        fwd_micro, grad_micro, doc_starts, fwd_resid[0], fwd_query[0], fwd_keyval[0],
        bwd_query[0], bwd_keyval[0], grad_in[0], out_weight[0],
    )
    return (out[None], gq[None], gkv[None], gw[None])


def solution(mesh):
    return jax.shard_map(
        shards,
        mesh=mesh,
        in_specs=(
            P("pipe", "tp", None),
            P("pipe", None, "tp"),
            P("pipe", None, None, "tp"),
            P("pipe"),
            P("pipe", None, "tp"),
            P("pipe", None, None, "tp"),
            P("pipe"),
            P("pipe", "tp", None),
            P("pipe", "tp", None),
            P(),
        ),
        out_specs=(
            P("pipe", "tp", None),
            P("pipe", None, "tp"),
            P("pipe", None, None, "tp"),
            P("pipe", "tp", None),
        ),
        check_vma=False,
    )
```

time: 185 us -> 69.5 us (0.38)
  waiting for transfers between devices: 101 us -> 0 us
  Pallas kernels: 0 us -> 57.2 us
  matrix products: 38.3 us -> 0 us
  starting transfers between devices: 14.3 us -> 0 us
  between operations: 14.3 us -> 1.93 us
  other arithmetic: 9.55 us -> 0 us
  local copies, waits for them, and re-layouts: 7.24 us -> 10.1 us
    ppermute x6 -> x0, waiting for transfers between devices: 80.9 us -> none  [from_behind(): return lax.ppermute(value, axis, pairs)]
    pallas_call x0 -> x1, Pallas kernels: none -> 57.2 us  [shards(): pl.pallas_call(kernel, out_shape=(jax.ShapeDtypeStruct((64, D), BF16), ja...]
    dot_general x11 -> x0, matrix products: 38.3 us -> none  [the longest x1 7.79 us: head_backward(): jnp.dot(grad_scores, key_head, preferred_element_type=jnp.float32)]
    reduce_scatter x1 -> x0, waiting for transfers between devices: 19.4 us -> none  [shards(): lax.psum_scatter(jnp.dot(attn_out, weight, preferred_element_type=jnp.flo...]
    ppermute x6 -> x0, starting transfers between devices: 14.2 us -> none  [from_behind(): return lax.ppermute(value, axis, pairs)]
    sub x2 -> x0, other arithmetic: 4.26 us -> none  [head_forward(): shifted = jnp.exp(scores - jnp.max(scores, axis=1, keepdims=True))]
    unnamed x14 -> x4, local copies, waits for them, and re-layouts: 6.16 us -> 10.1 us
    broadcast_in_dim x1 -> x0, other arithmetic: 1.96 us -> none  [shards(): phase_out[None]]
  transfers between devices with their start and end apart: 8 -> 0, of which waited for: 7 -> 0; matrix products, arithmetic and copies ran while one was open for 10% -> 0% of each run, Pallas kernels for 0% -> 0%
where the time goes in v1:
time: 69.5 us; the launch traced here: 69.2 us
  Pallas kernels  57.2 us (82%)
  local copies, waits for them, and re-layouts  10.1 us (15%)
  between operations  1.93 us (3%)
    pallas_call x1, Pallas kernels, shards(): pl.pallas_call(kernel, out_shape=(jax.ShapeDtypeStruct((64, D), BF16), ja...  57.2 us
    unnamed x4, local copies, waits for them, and re-layouts  10.1 us

profile of v1, /device:TPU:1, one launch (start us, length us, event | category | flops | bytes accessed | tf_op | source)
XLA Modules:
  0.0 69.2 jit_solution(7105805216601568522)
XLA Ops:
  1.9 57.2 %shard_map.129 = (bf16[64,4096]{1,0:T(8,128)(2,1)}, bf16[512,512]{1,0:T(8,128)(2,1)}, bf16[2,512,128]{2,1,0:T(8,128)(2,1)}, bf16[512,4096]{1,0:T(8,128)(2,1)}) custom-call(s32[1]{0:T(128)S(6)} %copy.18.fwd_micro, s32[1]{0:T(128)S(6)} %copy.19.grad_micro, s32[4,4]{1,0:T(4,128)} %starts.1, bf16[64,4096]{1,0:T(8,128)(2,1)} %bitcast.15, ...), custom_call_target="tpu_custom_call" | custom-call | tf_op jit(solution)/shard_map/pallas_call | solution.py:415
  59.1 1.9 %copy.20 = bf16[1,64,4096]{2,1,0:T(8,128)(2,1)} copy(bf16[1,64,4096]{2,1,0:T(8,128)(2,1)} %bitcast.14) | data formatting | bytes 1048576
  61.0 1.9 %copy.21 = bf16[1,512,512]{2,1,0:T(8,128)(2,1)} copy(bf16[1,512,512]{2,1,0:T(8,128)(2,1)} %bitcast.13) | data formatting | bytes 1048576
  62.8 1.7 %copy.22 = bf16[1,2,512,128]{3,2,1,0:T(8,128)(2,1)} copy(bf16[1,2,512,128]{3,2,1,0:T(8,128)(2,1)} %bitcast.19) | data formatting | bytes 524288
  64.5 4.7 %copy.23 = bf16[1,512,4096]{2,1,0:T(8,128)(2,1)} copy(bf16[1,512,4096]{2,1,0:T(8,128)(2,1)} %bitcast.12) | data formatting | bytes 8388608

commit v2 on v1

--- a/solution.py
+++ b/solution.py
@@ -200,9 +200,12 @@
         opp_copy(k).start()
 
     @pl.loop(0, 4)
-    def _(k):
-        from_next(k)
-        cols = pl.ds(pl.multiple_of(k * HD, HD), HD)
+    def _(h):
+        @pl.when(h == 3)
+        def _():
+            from_next(0)
+
+        cols = pl.ds(pl.multiple_of(h * HD, HD), HD)
         for b in range(2):
             n = 256 * (b + 1)
             rows = slice(256 * b, n)
@@ -210,16 +213,15 @@
             shifted = jnp.exp2((scores - jnp.max(scores, axis=0, keepdims=True)) * EXP_SCALE)
             total = jnp.sum(shifted, axis=0, keepdims=True)
             probs = (shifted * (1.0 / total)).astype(BF16)
-            pt_v[k, :n, rows] = probs
+            pt_v[h, :n, rows] = probs
             bat_v[cols, rows] = dot(vt_v[:, :n], probs).astype(BF16)
 
-        @pl.when(k >= 1)
-        def _():
-            from_sides(k - 1)
-
-        @pl.when(k >= 2)
-        def _():
-            from_opp(k - 2)
+    from_next(1)
+    from_sides(0)
+    from_next(2)
+    from_sides(1)
+    from_opp(0)
+    from_next(3)
 
     loads[4].wait()
     for h in range(4):
@@ -254,11 +256,16 @@
         window = pl.ds(pl.multiple_of(begin, TILE), TILE)
         return part[slot, core, :, window].astype(F32) + recvp[slot, :, window].astype(F32)
 
-    for pair in ((OPP, LEFT), (RIGHT, OWN)):
+    def project_pair(pair):
         for half in range(2):
             project(pair, (4 * half, 4 * half + 4))
             for slot in pair:
                 pp_copy(slot, half).start()
+
+    project_pair((OPP, LEFT))
+    from_sides(2)
+    project_pair((RIGHT, OWN))
+    from_opp(1)
 
     def opp_half(half):
         landed(recvp.at[OPP, :, halves[half]], pp_r.at[OPP, half])
@@ -275,10 +282,9 @@
     send_acc_l = rcopy(acc_l, fin_r.at[1], sl_s.at[2], sr_r.at[2], (pipe, left))
 
     opp_half(0)
+    opp_half(1)
     from_sides(3)
     send_opp_r.start()
-    opp_half(1)
-    from_opp(2)
     send_opp_l.start()
 
     def side_half(slot, half):
@@ -290,22 +296,30 @@
 
     side_half(LEFT, 0)
     side_half(RIGHT, 1)
-    from_opp(3)
     send_side_l.start()
     send_side_r.start()
 
-    for kind, shard in enumerate((tp + 1 - 2 * core, left + 1 - 2 * core, right + 1 - 2 * core, opp + 1 - 2 * core)):
-        for k in range(CHUNKS):
-            landed(g_v.at[rows_of(shard, k), :], p_r.at[kind, k])
-
-    acc_v[...] = jnp.zeros_like(acc_v)
-
-    @pl.loop(0, D // TILE)
-    def _(tile):
-        cols = pl.ds(pl.multiple_of(tile * TILE, TILE), TILE)
-        acc_v[...] += dot_nt(g_v[:, cols], w_v[:, cols])
-
-    ga_v[...] = acc_v[...].astype(BF16)
+    peer_shards = [lax.rem(shard, 8) + 1 - 2 * core for shard in (tp, left, right, opp)]
+
+    def attn_grad(half):
+        for k in (2 * half, 2 * half + 1):
+            for kind, shard in enumerate(peer_shards):
+                landed(g_v.at[rows_of(shard, k), :], p_r.at[kind, k])
+        acc_v[...] = jnp.zeros_like(acc_v)
+
+        @pl.loop(0, D // TILE)
+        def _(tile):
+            cols = pl.ds(pl.multiple_of(tile * TILE, TILE), TILE)
+            lhs = jnp.concatenate([g_v[64 * i + 32 * half : 64 * i + 32 * half + 32, cols] for i in range(8)], axis=0)
+            acc_v[...] += dot_nt(lhs, w_v[:, cols])
+
+        for i in range(8):
+            ga_v[64 * i + 32 * half : 64 * i + 32 * half + 32, :] = acc_v[32 * i : 32 * i + 32, :].astype(BF16)
+
+    attn_grad(0)
+    from_opp(2)
+    from_opp(3)
+    attn_grad(1)
 
     def gw_copy(tile):
         cols = pl.ds(pl.multiple_of(tile * TILE, TILE), TILE)
@@ -389,6 +403,21 @@
         store.wait()
 
 
+def deliver(*refs):
+    srcs, dsts, sem = refs[:4], refs[4:8], refs[8]
+    pieces = []
+    for src, dst in zip(srcs, dsts):
+        rows = src.shape[-2]
+        for lead in range(src.shape[0]):
+            for row in range(0, rows, 64):
+                pieces.append(tuple(ref.at[lead, pl.ds(row, 64), :] for ref in (src, dst)))
+    copies = [pltpu.make_async_copy(a, b, sem.at[i]) for i, (a, b) in enumerate(pieces)]
+    for copy in copies:
+        copy.start()
+    for copy in copies:
+        copy.wait()
+
+
 def shards(fwd_resid, fwd_query, fwd_keyval, fwd_micro, bwd_query, bwd_keyval, grad_micro, grad_in, out_weight, doc_starts):
     any_space = pl.BlockSpec(memory_space=pl.ANY)
     smem = pl.BlockSpec(memory_space=pltpu.SMEM)
@@ -400,7 +429,7 @@
         vmem((4, R, HD), BF16), vmem((4, R, HD), BF16), vmem((64, D), BF16),
         vmem((8, 128), jnp.int32), vmem((8, 128), jnp.int32),
         vmem((R, R), F32), vmem((R, R), F32), vmem((HD, R), BF16), vmem((HD, R), BF16),
-        vmem((4, R, R), BF16), vmem((R, R), BF16), vmem((R, R), F32), vmem((R, R), BF16),
+        vmem((4, R, R), BF16), vmem((R, R), BF16), vmem((R // 2, R), F32), vmem((R, R), BF16),
         vmem((R, HD), F32), vmem((R, HD), F32), vmem((R, R), BF16), vmem((2, R, HD), BF16), vmem((R, D), BF16),
         vmem((4, 2, 64, D), BF16), vmem((4, 64, D), BF16), vmem((2, 64, HALF), BF16), vmem((2, 64, HALF), BF16),
         vmem((64, HALF), BF16), vmem((64, HALF), BF16), vmem((2, 64, HALF), BF16), vmem((2, 64, HALF), BF16),
@@ -420,17 +449,30 @@
             jax.ShapeDtypeStruct((2, R, HD), BF16),
             jax.ShapeDtypeStruct((R, D), BF16),
         ),
-        in_specs=[smem] * 3 + [any_space] * 7,
+        in_specs=[smem] * 3 + [pl.BlockSpec(memory_space=pltpu.HBM)] * 7,
         out_specs=(any_space,) * 4,
         scratch_shapes=scratch,
         compiler_params=pltpu.CompilerParams(
-            collective_id=0, has_side_effects=True, vmem_limit_bytes=60 * 1024 * 1024
+            collective_id=0, has_side_effects=True, vmem_limit_bytes=40 * 1024 * 1024
         ),
     )(
-        fwd_micro, grad_micro, doc_starts, fwd_resid[0], fwd_query[0], fwd_keyval[0],
-        bwd_query[0], bwd_keyval[0], grad_in[0], out_weight[0],
+        fwd_micro, grad_micro, pltpu.with_memory_space_constraint(doc_starts, pltpu.HBM),
+        *(
+            pltpu.with_memory_space_constraint(a[0], pltpu.HBM)
+            for a in (fwd_resid, fwd_query, fwd_keyval, bwd_query, bwd_keyval, grad_in, out_weight)
+        ),
     )
-    return (out[None], gq[None], gkv[None], gw[None])
+    arrays = (gw[None], gq[None], gkv, out[None])
+    count = sum(a.shape[0] * max(a.shape[1] // 64, 1) for a in arrays)
+    gw, gq, gkv, out = pl.pallas_call(
+        deliver,
+        out_shape=tuple(jax.ShapeDtypeStruct(a.shape, a.dtype) for a in arrays),
+        in_specs=[any_space] * 4,
+        out_specs=(any_space,) * 4,
+        scratch_shapes=[dma((count,))],
+        compiler_params=pltpu.CompilerParams(vmem_limit_bytes=4 * 1024 * 1024),
+    )(*arrays)
+    return (out, gq, gkv[None], gw)
 
 
 def solution(mesh):

time: 69.5 us -> 61.4 us (0.88)
  local copies, waits for them, and re-layouts: 10.1 us -> 0 us
  Pallas kernels: 57.2 us -> 59.4 us
    unnamed x4 -> x0, local copies, waits for them, and re-layouts: 10.1 us -> none
    pallas_call x0 -> x1, Pallas kernels: none -> 2.7 us  [shards(): pl.pallas_call(deliver, out_shape=tuple((jax.ShapeDtypeStruct(a.shape, a....]
where the time goes in v2:
time: 61.4 us; the launch traced here: 61.3 us
  Pallas kernels  59.4 us (97%)
  between operations  1.93 us (3%)
    pallas_call x1, Pallas kernels, shards(): pl.pallas_call(kernel, out_shape=(jax.ShapeDtypeStruct((64, D), BF16), ja...  56.7 us
    pallas_call x1, Pallas kernels, shards(): pl.pallas_call(deliver, out_shape=tuple((jax.ShapeDtypeStruct(a.shape, a....  2.7 us

profile of v2, /device:TPU:1, one launch (start us, length us, event | category | flops | bytes accessed | tf_op | source)
XLA Modules:
  0.0 61.3 jit_solution(10419384034416556906)
XLA Ops:
  1.9 56.7 %shard_map.129 = (bf16[64,4096]{1,0:T(8,128)(2,1)S(1)}, bf16[512,512]{1,0:T(8,128)(2,1)S(1)}, bf16[2,512,128]{2,1,0:T(8,128)(2,1)S(1)}, bf16[512,4096]{1,0:T(8,128)(2,1)S(1)}) custom-call(s32[1]{0:T(128)S(6)} %copy.14.fwd_micro, s32[1]{0:T(128)S(6)} %copy.15.grad_micro, s32[4,4]{1,0:T(4,128)} %starts.1, bf16[64,4096]{1,0:T(8,128)(2,1)} %bitcast.15, ...), custom_call_target="tpu_custom_call" | custom-call | tf_op jit(solution)/shard_map/pallas_call | solution.py:444
  58.6 2.7 %shard_map.130 = (bf16[1,512,4096]{2,1,0:T(8,128)(2,1)}, bf16[1,512,512]{2,1,0:T(8,128)(2,1)}, bf16[2,512,128]{2,1,0:T(8,128)(2,1)}, bf16[1,64,4096]{2,1,0:T(8,128)(2,1)}) custom-call(bf16[1,512,4096]{2,1,0:T(8,128)(2,1)S(1)} %bitcast.11, bf16[1,512,512]{2,1,0:T(8,128)(2,1)S(1)} %bitcast.13, bf16[2,512,128]{2,1,0:T(8,128)(2,1)S(1)} %get-tuple-element.14.refs_2_, ...), custom_call_target="tpu_custom_call" | custom-call | tf_op jit(solution)/shard_map/pallas_call | solution.py:467

commit v3 on v2

--- a/solution.py
+++ b/solution.py
@@ -21,7 +21,10 @@
 CHUNKS = 4
 CROWS = 64 // CHUNKS
 TILE = 512
-OPP, LEFT, RIGHT, OWN = 0, 1, 2, 3
+DEEP = 1024
+PIECES = ((0, 0, HALF), (0, HALF, HALF), (1, 0, D), (2, 0, D), (3, 0, D))
+LAST = len(PIECES) - 1
+OPP, LEFT, OWN, RIGHT = 0, 1, 2, 3
 
 
 def dot(a, b):
@@ -36,9 +39,10 @@
     fwd_micro, grad_micro, starts, resid, fq, fkv, bq, bkv, grad, weight,
     out, gq, gkv, gw,
     fq_v, fkv_v, bq_v, bkv_v, w_v, g_v, attn_out, attn_in, resid_in, mic_out, mic_in,
-    bias_f, bias_b, kt_v, vt_v, pt_v, bat_v, acc_v, ga_v, dk_v, dv_v, gq_v, gkv_v, gw_v,
+    bias_b, kt_v, vt_v, pt_v, bat_v, acc_v, ga_v, dk_v, dv_v, gq_v, gkv_v, gw_v,
     part, recvp, opp_sum, side_sum, rel_l, rel_r, fin_l, fin_r, acc_r, acc_l, out_v,
     ld_sem, st_sem, gw_sem,
+    early_l, early_r, el_s, el_r, er_s, er_r, ez_s, ez_r,
     z_s, z_r, mic_s, mic_r, at_s, at_r, rs_s, rs_r,
     xr_s, xl_s, fl_r, fr_r, yr_s, yl_s, fl2_r, fr2_r, p_s, p_r,
     pp_s, pp_r, sr_s, sl_s, sl_r, sr_r,
@@ -78,52 +82,63 @@
     for m in range(1, 4):
         first = [jnp.where(fwd_micro[0] == m, starts[m, d], first[d]) for d in range(4)]
 
+    pl.semaphore_wait(barrier, len(peers))
+
+    def rows_of(shard, k):
+        return pl.ds(pl.multiple_of(shard * 64 + k * CROWS, CROWS), CROWS)
+
+    def view(shard, p):
+        chunk, first_col, cols = PIECES[p]
+        return g_v.at[rows_of(shard, chunk), pl.ds(first_col, cols)]
+
+    def z_copy(p):
+        chunk, first_col, cols = PIECES[p]
+        mine = grad.at[pl.ds(chunk * CROWS, CROWS), pl.ds(first_col, cols)]
+        return rcopy(mine, view(tp, p), z_s.at[p], z_r.at[p], (prv, tp))
+
+    mic = rcopy(mic_out, mic_in, mic_s, mic_r, (prv, tp))
+    mic.start()
+    for p in range(LAST):
+        z_copy(p).start()
+
+    last_rows = grad.at[pl.ds(3 * CROWS, CROWS), :]
+    early_to_r = rcopy(last_rows, early_l, er_s, el_r, (pipe, right))
+    early_to_l = rcopy(last_rows, early_r, el_s, er_r, (pipe, left))
+    early_to_r.start()
+    early_to_l.start()
+    early_z_l = rcopy(early_l, view(left, LAST), ez_s.at[0], ez_r.at[0], (prv, tp))
+    early_z_r = rcopy(early_r, view(right, LAST), ez_s.at[1], ez_r.at[1], (prv, tp))
+
+    loads[0].wait()
+    loads[1].wait()
+
+    def attn_copy(slot):
+        return rcopy(attn_out.at[slot], attn_in.at[slot], at_s.at[slot], at_r.at[slot], (nxt, tp))
+
     @pl.loop(0, 4)
-    def _(block):
-        row0 = pl.multiple_of(block * 128, 128)
+    def _(slot):
+        row0 = pl.multiple_of(lax.rem(chip + slot + 2, 4) * 128, 128)
         row = lax.broadcasted_iota(jnp.int32, (128, R), 0) + row0
         column = lax.broadcasted_iota(jnp.int32, (128, R), 1)
         begin = jnp.zeros((128, R), jnp.int32)
         for d in range(4):
             begin = jnp.maximum(begin, jnp.where(row >= first[d], first[d], 0))
-        bias_f[pl.ds(row0, 128), :] = jnp.where((column >= begin) & (column <= row), 0.0, MASKED)
-
-    pl.semaphore_wait(barrier, len(peers))
-
-    def rows_of(shard, k):
-        return pl.ds(pl.multiple_of(shard * 64 + k * CROWS, CROWS), CROWS)
-
-    def z_copy(k):
-        return rcopy(
-            grad.at[pl.ds(pl.multiple_of(k * CROWS, CROWS), CROWS), :], g_v.at[rows_of(tp, k), :],
-            z_s.at[k], z_r.at[k], (prv, tp),
-        )
-
-    mic = rcopy(mic_out, mic_in, mic_s, mic_r, (prv, tp))
-    mic.start()
-    for k in range(CHUNKS):
-        z_copy(k).start()
-
-    loads[0].wait()
-    loads[1].wait()
-
-    def attn_copy(h):
-        return rcopy(attn_out.at[h], attn_in.at[h], at_s.at[h], at_r.at[h], (nxt, tp))
-
-    @pl.loop(0, 4)
-    def _(h):
-        cols = pl.ds(pl.multiple_of(h * HD, HD), HD)
-        for b in range(2):
-            n = 256 * (b + 1)
-            rows = slice(256 * b, n)
-            scores = dot_nt(fq_v[rows, cols], fkv_v[0, :n, :]) + bias_f[rows, :n]
+        bias = jnp.where((column >= begin) & (column <= row), 0.0, MASKED)
+        for h in range(4):
+            cols = slice(HD * h, HD * h + HD)
+            scores = dot_nt(fq_v[pl.ds(row0, 128), cols], fkv_v[0]) + bias
             shifted = jnp.exp2((scores - jnp.max(scores, axis=1, keepdims=True)) * EXP_SCALE)
             total = jnp.sum(shifted, axis=1, keepdims=True)
-            attn_out[h, rows, :] = (dot(shifted.astype(BF16), fkv_v[1, :n, :]) * (1.0 / total)).astype(BF16)
-        attn_copy(h).start()
+            attn_out[slot, :, cols] = (dot(shifted.astype(BF16), fkv_v[1]) * (1.0 / total)).astype(BF16)
+        attn_copy(slot).start()
 
     resid_copy = rcopy(resid, resid_in, rs_s, rs_r, (nxt, tp))
     resid_copy.start()
+    early_to_r.wait_recv()
+    early_z_l.start()
+    early_to_l.wait_recv()
+    early_z_r.start()
+    z_copy(LAST).start()
 
     loads[2].wait()
     loads[3].wait()
@@ -153,57 +168,76 @@
 
     half_a, half_b = pl.ds(0, HALF), pl.ds(HALF, HALF)
 
-    def x_copies(k):
-        mine = g_v.at[rows_of(tp, k), :]
-        return (
-            rcopy(mine, mine, xr_s.at[k], fl_r.at[k], (pipe, right)),
-            rcopy(mine, mine, xl_s.at[k], fr_r.at[k], (pipe, left)),
-            rcopy(mine, mine, p_s.at[0, k], p_r.at[0, k], (pipe, partner)),
-        )
-
-    def left_copies(k):
-        theirs = g_v.at[rows_of(left, k), half_a]
-        whole = g_v.at[rows_of(left, k), :]
-        return (
-            rcopy(theirs, theirs, yr_s.at[k], fl2_r.at[k], (pipe, right)),
-            rcopy(whole, whole, p_s.at[1, k], p_r.at[1, k], (pipe, partner)),
-        )
-
-    def right_copies(k):
-        theirs = g_v.at[rows_of(right, k), half_b]
-        whole = g_v.at[rows_of(right, k), :]
-        return (
-            rcopy(theirs, theirs, yl_s.at[k], fr2_r.at[k], (pipe, left)),
-            rcopy(whole, whole, p_s.at[2, k], p_r.at[2, k], (pipe, partner)),
-        )
+    def to_partner(kind, p, ref):
+        return rcopy(ref, ref, p_s.at[kind, p], p_r.at[kind, p], (pipe, partner))
+
+    def x_copies(p, with_chips=True):
+        mine = view(tp, p)
+        beside = (
+            rcopy(mine, mine, xr_s.at[p], fl_r.at[p], (pipe, right)),
+            rcopy(mine, mine, xl_s.at[p], fr_r.at[p], (pipe, left)),
+        ) if with_chips else ()
+        return (*beside, to_partner(0, p, mine))
+
+    def left_copies(p):
+        chunk = PIECES[p][0]
+        theirs = g_v.at[rows_of(left, chunk), half_a]
+        onward = (rcopy(theirs, theirs, yr_s.at[chunk], fl2_r.at[chunk], (pipe, right)),) if p != 1 else ()
+        return (*onward, to_partner(1, p, view(left, p)))
+
+    def right_copies(p):
+        chunk = PIECES[p][0]
+        theirs = g_v.at[rows_of(right, chunk), half_b]
+        onward = (rcopy(theirs, theirs, yl_s.at[chunk], fr2_r.at[chunk], (pipe, left)),) if p != 0 else ()
+        return (*onward, to_partner(2, p, view(right, p)))
 
     def opp_copy(k):
-        whole = g_v.at[rows_of(opp, k), :]
-        return rcopy(whole, whole, p_s.at[3, k], p_r.at[3, k], (pipe, partner))
-
-    def from_next(k):
-        landed(g_v.at[rows_of(tp, k), :], z_r.at[k])
-        for copy in x_copies(k):
+        return to_partner(3, k, g_v.at[rows_of(opp, k), :])
+
+    def start_all(copies):
+        for copy in copies:
             copy.start()
 
-    def from_sides(k):
-        landed(g_v.at[rows_of(left, k), :], fl_r.at[k])
-        for copy in left_copies(k):
-            copy.start()
-        landed(g_v.at[rows_of(right, k), :], fr_r.at[k])
-        for copy in right_copies(k):
-            copy.start()
+    def from_next(p):
+        landed(view(tp, p), z_r.at[p])
+        start_all(x_copies(p))
+
+    def from_sides(p):
+        landed(view(left, p), fl_r.at[p])
+        start_all(left_copies(p))
+        landed(view(right, p), fr_r.at[p])
+        start_all(right_copies(p))
 
     def from_opp(k):
         landed(g_v.at[rows_of(opp, k), half_a], fl2_r.at[k])
         landed(g_v.at[rows_of(opp, k), half_b], fr2_r.at[k])
         opp_copy(k).start()
 
+    def last_left():
+        early_z_l.wait_recv()
+        start_all(left_copies(LAST))
+
+    def last_right():
+        early_z_r.wait_recv()
+        start_all(right_copies(LAST))
+
+    def last_own():
+        landed(view(tp, LAST), z_r.at[LAST])
+        start_all(x_copies(LAST, False))
+
     @pl.loop(0, 4)
     def _(h):
+        @pl.when(h == 0)
+        def _():
+            from_next(0)
+
+        @pl.when(h == 2)
+        def _():
+            from_next(1)
+
         @pl.when(h == 3)
         def _():
-            from_next(0)
+            from_sides(0)
 
         cols = pl.ds(pl.multiple_of(h * HD, HD), HD)
         for b in range(2):
@@ -216,26 +250,15 @@
             pt_v[h, :n, rows] = probs
             bat_v[cols, rows] = dot(vt_v[:, :n], probs).astype(BF16)
 
-    from_next(1)
-    from_sides(0)
     from_next(2)
     from_sides(1)
-    from_opp(0)
-    from_next(3)
 
     loads[4].wait()
-    for h in range(4):
-        landed(attn_in.at[h], at_r.at[h])
-    chip_of = (lax.rem(chip + 2, 4), lax.rem(chip + 3, 4), lax.rem(chip + 1, 4), chip)
-
-    def project(pair, tiles):
-        def block(slot):
-            rows = pl.ds(pl.multiple_of(chip_of[slot] * 128, 128), 128)
-            return jnp.concatenate([attn_in[h, rows, :] for h in range(4)], axis=1)
-
-        lhs = jnp.concatenate([block(slot) for slot in pair], axis=0)
-
-        @pl.loop(tiles[0], tiles[1])
+
+    def project(pair, half):
+        lhs = jnp.concatenate([attn_in[slot] for slot in pair], axis=0)
+
+        @pl.loop(4 * half, 4 * half + 4)
         def _(tile):
             cols = pl.ds(pl.multiple_of(tile * TILE, TILE), TILE)
             product = dot(lhs, w_v[:, cols]).astype(BF16)
@@ -243,6 +266,9 @@
                 for c in range(2):
                     part[slot, c, :, cols] = product[128 * i + 64 * c : 128 * i + 64 * c + 64, :]
 
+        for slot in pair:
+            pp_copy(slot, half).start()
+
     halves = (half_a, half_b)
 
     def pp_copy(slot, half):
@@ -255,17 +281,6 @@
         begin = half * HALF + cols
         window = pl.ds(pl.multiple_of(begin, TILE), TILE)
         return part[slot, core, :, window].astype(F32) + recvp[slot, :, window].astype(F32)
-
-    def project_pair(pair):
-        for half in range(2):
-            project(pair, (4 * half, 4 * half + 4))
-            for slot in pair:
-                pp_copy(slot, half).start()
-
-    project_pair((OPP, LEFT))
-    from_sides(2)
-    project_pair((RIGHT, OWN))
-    from_opp(1)
 
     def opp_half(half):
         landed(recvp.at[OPP, :, halves[half]], pp_r.at[OPP, half])
@@ -281,12 +296,6 @@
     send_acc_r = rcopy(acc_r, fin_l.at[0], sr_s.at[2], sl_r.at[2], (pipe, right))
     send_acc_l = rcopy(acc_l, fin_r.at[1], sl_s.at[2], sr_r.at[2], (pipe, left))
 
-    opp_half(0)
-    opp_half(1)
-    from_sides(3)
-    send_opp_r.start()
-    send_opp_l.start()
-
     def side_half(slot, half):
         landed(recvp.at[slot, :, halves[half]], pp_r.at[slot, half])
 
@@ -294,22 +303,45 @@
         def _(cols):
             side_sum[half, :, pl.ds(pl.multiple_of(cols, TILE), TILE)] = chip_sum(slot, half, cols).astype(BF16)
 
+    def landed_attn(pair):
+        for slot in pair:
+            landed(attn_in.at[slot], at_r.at[slot])
+
+    near, far = (OWN, RIGHT), (OPP, LEFT)
+    landed_attn(far)
+    project(far, 0)
+    from_next(3)
+    project(far, 1)
+    from_sides(2)
+    from_opp(0)
+    opp_half(0)
+    opp_half(1)
+    last_left()
+    landed_attn(near)
+    project(near, 0)
+    from_sides(3)
+    send_opp_r.start()
+    project(near, 1)
+    last_right()
+    send_opp_l.start()
     side_half(LEFT, 0)
-    side_half(RIGHT, 1)
     send_side_l.start()
-    send_side_r.start()
+    from_opp(1)
 
     peer_shards = [lax.rem(shard, 8) + 1 - 2 * core for shard in (tp, left, right, opp)]
 
     def attn_grad(half):
         for k in (2 * half, 2 * half + 1):
-            for kind, shard in enumerate(peer_shards):
-                landed(g_v.at[rows_of(shard, k), :], p_r.at[kind, k])
+            for kind, shard in enumerate(peer_shards[:3]):
+                for p in range(len(PIECES)):
+                    if PIECES[p][0] == k:
+                        landed(view(shard, p), p_r.at[kind, p])
+            landed(g_v.at[rows_of(peer_shards[3], k), :], p_r.at[3, k])
         acc_v[...] = jnp.zeros_like(acc_v)
 
-        @pl.loop(0, D // TILE)
+        @pl.loop(0, D // DEEP)
         def _(tile):
-            cols = pl.ds(pl.multiple_of(tile * TILE, TILE), TILE)
+            cols = pl.ds(pl.multiple_of(tile * DEEP, DEEP), DEEP)
             lhs = jnp.concatenate([g_v[64 * i + 32 * half : 64 * i + 32 * half + 32, cols] for i in range(8)], axis=0)
             acc_v[...] += dot_nt(lhs, w_v[:, cols])
 
@@ -317,6 +349,9 @@
             ga_v[64 * i + 32 * half : 64 * i + 32 * half + 32, :] = acc_v[32 * i : 32 * i + 32, :].astype(BF16)
 
     attn_grad(0)
+    side_half(RIGHT, 1)
+    send_side_r.start()
+    last_own()
     from_opp(2)
     from_opp(3)
     attn_grad(1)
@@ -325,11 +360,14 @@
         cols = pl.ds(pl.multiple_of(tile * TILE, TILE), TILE)
         return pltpu.make_async_copy(gw_v.at[:, cols], gw.at[:, cols], gw_sem.at[tile])
 
-    @pl.loop(0, D // TILE)
-    def _(tile):
-        cols = pl.ds(pl.multiple_of(tile * TILE, TILE), TILE)
-        gw_v[:, cols] = dot(bat_v[...], g_v[:, cols]).astype(BF16)
-        gw_copy(tile).start()
+    def weight_grad(half):
+        @pl.loop(4 * half, 4 * half + 4)
+        def _(tile):
+            cols = pl.ds(pl.multiple_of(tile * TILE, TILE), TILE)
+            gw_v[:, cols] = dot(bat_v[...], g_v[:, cols]).astype(BF16)
+            gw_copy(tile).start()
+
+    weight_grad(0)
 
     landed(rel_l, sl_r.at[0])
     landed(recvp.at[RIGHT, :, half_a], pp_r.at[RIGHT, 0])
@@ -344,6 +382,8 @@
 
     send_acc_r.start()
     send_acc_l.start()
+
+    weight_grad(1)
 
     @pl.loop(0, 4)
     def _(h):
@@ -388,10 +428,13 @@
     resid_copy.wait_send()
     for h in range(4):
         attn_copy(h).wait_send()
+    for copy in (early_to_r, early_to_l, early_z_l, early_z_r):
+        copy.wait_send()
+    for p in range(len(PIECES)):
+        for copy in (z_copy(p), *x_copies(p, p < LAST), *left_copies(p), *right_copies(p)):
+            copy.wait_send()
     for k in range(CHUNKS):
-        z_copy(k).wait_send()
-        for copy in (*x_copies(k), *left_copies(k), *right_copies(k), opp_copy(k)):
-            copy.wait_send()
+        opp_copy(k).wait_send()
     for slot in range(4):
         for half in range(2):
             pp_copy(slot, half).wait_send()
@@ -426,19 +469,20 @@
     scratch = [
         vmem((R, R), BF16), vmem((2, R, HD), BF16), vmem((R, R), BF16), vmem((2, R, HD), BF16),
         vmem((R, D), BF16), vmem((R, D), BF16),
-        vmem((4, R, HD), BF16), vmem((4, R, HD), BF16), vmem((64, D), BF16),
+        vmem((4, HD, R), BF16), vmem((4, HD, R), BF16), vmem((64, D), BF16),
         vmem((8, 128), jnp.int32), vmem((8, 128), jnp.int32),
-        vmem((R, R), F32), vmem((R, R), F32), vmem((HD, R), BF16), vmem((HD, R), BF16),
+        vmem((R, R), F32), vmem((HD, R), BF16), vmem((HD, R), BF16),
         vmem((4, R, R), BF16), vmem((R, R), BF16), vmem((R // 2, R), F32), vmem((R, R), BF16),
         vmem((R, HD), F32), vmem((R, HD), F32), vmem((R, R), BF16), vmem((2, R, HD), BF16), vmem((R, D), BF16),
         vmem((4, 2, 64, D), BF16), vmem((4, 64, D), BF16), vmem((2, 64, HALF), BF16), vmem((2, 64, HALF), BF16),
         vmem((64, HALF), BF16), vmem((64, HALF), BF16), vmem((2, 64, HALF), BF16), vmem((2, 64, HALF), BF16),
         vmem((64, HALF), BF16), vmem((64, HALF), BF16), vmem((64, D), BF16),
         dma((5,)), dma((4,)), dma((D // TILE,)),
-        dma((CHUNKS,)), dma((CHUNKS,)), dma, dma, dma((4,)), dma((4,)), dma, dma,
+        vmem((CROWS, D), BF16), vmem((CROWS, D), BF16), dma, dma, dma, dma, dma((2,)), dma((2,)),
+        dma((len(PIECES),)), dma((len(PIECES),)), dma, dma, dma((4,)), dma((4,)), dma, dma,
+        dma((LAST,)), dma((LAST,)), dma((LAST,)), dma((LAST,)),
         dma((CHUNKS,)), dma((CHUNKS,)), dma((CHUNKS,)), dma((CHUNKS,)),
-        dma((CHUNKS,)), dma((CHUNKS,)), dma((CHUNKS,)), dma((CHUNKS,)),
-        dma((4, CHUNKS)), dma((4, CHUNKS)),
+        dma((4, len(PIECES))), dma((4, len(PIECES))),
         dma((4, 2)), dma((4, 2)), dma((3,)), dma((3,)), dma((3,)), dma((3,)),
     ]
     out, gq, gkv, gw = pl.pallas_call(

time: 61.4 us -> 56.5 us (0.920)
  Pallas kernels: 59.4 us -> 54.4 us
    pallas_call x1, Pallas kernels: 56.7 us -> 51.7 us  [shards(): pl.pallas_call(kernel, out_shape=(jax.ShapeDtypeStruct((64, D), BF16), ja...]
where the time goes in v3:
time: 56.5 us; the launch traced here: 56.3 us
  Pallas kernels  54.4 us (96%)
  between operations  1.93 us (3%)
    pallas_call x1, Pallas kernels, shards(): pl.pallas_call(kernel, out_shape=(jax.ShapeDtypeStruct((64, D), BF16), ja...  51.7 us
    pallas_call x1, Pallas kernels, shards(): pl.pallas_call(deliver, out_shape=tuple((jax.ShapeDtypeStruct(a.shape, a....  2.7 us

profile of v3, /device:TPU:1, one launch (start us, length us, event | category | flops | bytes accessed | tf_op | source)
XLA Modules:
  0.0 56.3 jit_solution(3941289896816930695)
XLA Ops:
  1.9 51.7 %shard_map.129 = (bf16[64,4096]{1,0:T(8,128)(2,1)S(1)}, bf16[512,512]{1,0:T(8,128)(2,1)S(1)}, bf16[2,512,128]{2,1,0:T(8,128)(2,1)S(1)}, bf16[512,4096]{1,0:T(8,128)(2,1)S(1)}) custom-call(s32[1]{0:T(128)S(6)} %copy.14.fwd_micro, s32[1]{0:T(128)S(6)} %copy.15.grad_micro, s32[4,4]{1,0:T(4,128)} %starts.1, bf16[64,4096]{1,0:T(8,128)(2,1)} %bitcast.15, ...), custom_call_target="tpu_custom_call" | custom-call | tf_op jit(solution)/shard_map/pallas_call | solution.py:488
  53.6 2.7 %shard_map.130 = (bf16[1,512,4096]{2,1,0:T(8,128)(2,1)}, bf16[1,512,512]{2,1,0:T(8,128)(2,1)}, bf16[2,512,128]{2,1,0:T(8,128)(2,1)}, bf16[1,64,4096]{2,1,0:T(8,128)(2,1)}) custom-call(bf16[1,512,4096]{2,1,0:T(8,128)(2,1)S(1)} %bitcast.11, bf16[1,512,512]{2,1,0:T(8,128)(2,1)S(1)} %bitcast.13, bf16[2,512,128]{2,1,0:T(8,128)(2,1)S(1)} %get-tuple-element.14.refs_2_, ...), custom_call_target="tpu_custom_call" | custom-call | tf_op jit(solution)/shard_map/pallas_call | solution.py:511

commit v4 on v3

--- a/solution.py
+++ b/solution.py
@@ -36,13 +36,13 @@
 
 
 def kernel(
-    fwd_micro, grad_micro, starts, resid, fq, fkv, bq, bkv, grad, weight,
+    fwd_micro, grad_micro, starts_h, resid, fq, fkv, bq, bkv, grad, weight,
     out, gq, gkv, gw,
-    fq_v, fkv_v, bq_v, bkv_v, w_v, g_v, attn_out, attn_in, resid_in, mic_out, mic_in,
+    starts, fq_v, fkv_v, bq_v, bkv_v, w_v, g_v, attn_out, attn_in, resid_in, mic_out, mic_in,
     bias_b, kt_v, vt_v, pt_v, bat_v, acc_v, ga_v, dk_v, dv_v, gq_v, gkv_v, gw_v,
     part, recvp, opp_sum, side_sum, rel_l, rel_r, fin_l, fin_r, acc_r, acc_l, out_v,
     ld_sem, st_sem, gw_sem,
-    early_l, early_r, el_s, el_r, er_s, er_r, ez_s, ez_r,
+    early_l, early_r, early_o, el_s, el_r, er_s, er_r, eo_s, eo_r, ez_s, ez_r,
     z_s, z_r, mic_s, mic_r, at_s, at_r, rs_s, rs_r,
     xr_s, xl_s, fl_r, fr_r, yr_s, yl_s, fl2_r, fr2_r, p_s, p_r,
     pp_s, pp_r, sr_s, sl_s, sl_r, sr_r,
@@ -66,17 +66,21 @@
     loads = [
         pltpu.make_async_copy(src, dst, ld_sem.at[i])
         for i, (src, dst) in enumerate(
-            [(fkv, fkv_v), (fq, fq_v), (bkv, bkv_v), (bq, bq_v), (weight, w_v)]
+            [
+                (fkv, fkv_v), (fq, fq_v), (bkv, bkv_v), (bq, bq_v), (weight, w_v),
+                (starts_h, starts),
+            ]
         )
     ]
-    for load in loads:
-        load.start()
-    mic_out[...] = jnp.full(mic_out.shape, grad_micro[0], jnp.int32)
-
     barrier = pltpu.get_barrier_semaphore()
     peers = ((pipe, partner), (pipe, right), (pipe, left), (nxt, tp), (prv, tp))
     for peer in peers:
         pl.semaphore_signal(barrier, inc=1, device_id=peer, device_id_type=MESH)
+    for load in (*loads[5:], *loads[:5]):
+        load.start()
+    for load in loads[5:]:
+        load.wait()
+    mic_out[...] = jnp.full(mic_out.shape, grad_micro[0], jnp.int32)
 
     first = [starts[0, d] for d in range(4)]
     for m in range(1, 4):
@@ -108,6 +112,10 @@
     early_to_l.start()
     early_z_l = rcopy(early_l, view(left, LAST), ez_s.at[0], ez_r.at[0], (prv, tp))
     early_z_r = rcopy(early_r, view(right, LAST), ez_s.at[1], ez_r.at[1], (prv, tp))
+    early_z_o = rcopy(early_o, view(opp, LAST), ez_s.at[2], ez_r.at[2], (prv, tp))
+    half_a, half_b = pl.ds(0, HALF), pl.ds(HALF, HALF)
+    onward_r = rcopy(early_l.at[:, half_a], early_o.at[:, half_a], eo_s.at[0], eo_r.at[0], (pipe, right))
+    onward_l = rcopy(early_r.at[:, half_b], early_o.at[:, half_b], eo_s.at[1], eo_r.at[1], (pipe, left))
 
     loads[0].wait()
     loads[1].wait()
@@ -134,12 +142,6 @@
 
     resid_copy = rcopy(resid, resid_in, rs_s, rs_r, (nxt, tp))
     resid_copy.start()
-    early_to_r.wait_recv()
-    early_z_l.start()
-    early_to_l.wait_recv()
-    early_z_r.start()
-    z_copy(LAST).start()
-
     loads[2].wait()
     loads[3].wait()
     mic.wait_recv()
@@ -166,8 +168,6 @@
     dk_v[...] = jnp.zeros_like(dk_v)
     dv_v[...] = jnp.zeros_like(dv_v)
 
-    half_a, half_b = pl.ds(0, HALF), pl.ds(HALF, HALF)
-
     def to_partner(kind, p, ref):
         return rcopy(ref, ref, p_s.at[kind, p], p_r.at[kind, p], (pipe, partner))
 
@@ -182,13 +182,13 @@
     def left_copies(p):
         chunk = PIECES[p][0]
         theirs = g_v.at[rows_of(left, chunk), half_a]
-        onward = (rcopy(theirs, theirs, yr_s.at[chunk], fl2_r.at[chunk], (pipe, right)),) if p != 1 else ()
+        onward = (rcopy(theirs, theirs, yr_s.at[chunk], fl2_r.at[chunk], (pipe, right)),) if p not in (1, LAST) else ()
         return (*onward, to_partner(1, p, view(left, p)))
 
     def right_copies(p):
         chunk = PIECES[p][0]
         theirs = g_v.at[rows_of(right, chunk), half_b]
-        onward = (rcopy(theirs, theirs, yl_s.at[chunk], fr2_r.at[chunk], (pipe, left)),) if p != 0 else ()
+        onward = (rcopy(theirs, theirs, yl_s.at[chunk], fr2_r.at[chunk], (pipe, left)),) if p not in (0, LAST) else ()
         return (*onward, to_partner(2, p, view(right, p)))
 
     def opp_copy(k):
@@ -221,6 +221,10 @@
         early_z_r.wait_recv()
         start_all(right_copies(LAST))
 
+    def last_opp():
+        early_z_o.wait_recv()
+        opp_copy(CHUNKS - 1).start()
+
     def last_own():
         landed(view(tp, LAST), z_r.at[LAST])
         start_all(x_copies(LAST, False))
@@ -231,13 +235,19 @@
         def _():
             from_next(0)
 
+        @pl.when(h == 1)
+        def _():
+            early_to_r.wait_recv()
+            onward_r.start()
+            early_z_l.start()
+            early_to_l.wait_recv()
+            onward_l.start()
+            early_z_r.start()
+            z_copy(LAST).start()
+
         @pl.when(h == 2)
         def _():
             from_next(1)
-
-        @pl.when(h == 3)
-        def _():
-            from_sides(0)
 
         cols = pl.ds(pl.multiple_of(h * HD, HD), HD)
         for b in range(2):
@@ -251,7 +261,9 @@
             bat_v[cols, rows] = dot(vt_v[:, :n], probs).astype(BF16)
 
     from_next(2)
+    from_sides(0)
     from_sides(1)
+    from_next(3)
 
     loads[4].wait()
 
@@ -310,7 +322,9 @@
     near, far = (OWN, RIGHT), (OPP, LEFT)
     landed_attn(far)
     project(far, 0)
-    from_next(3)
+    onward_r.wait_recv()
+    onward_l.wait_recv()
+    early_z_o.start()
     project(far, 1)
     from_sides(2)
     from_opp(0)
@@ -348,26 +362,36 @@
         for i in range(8):
             ga_v[64 * i + 32 * half : 64 * i + 32 * half + 32, :] = acc_v[32 * i : 32 * i + 32, :].astype(BF16)
 
-    attn_grad(0)
+
+    @pl.when(core == 1)
+    def _():
+        from_opp(2)
+        last_own()
+
     side_half(RIGHT, 1)
     send_side_r.start()
-    last_own()
-    from_opp(2)
-    from_opp(3)
+    attn_grad(0)
+
+    @pl.when(core == 0)
+    def _():
+        last_own()
+        from_opp(2)
+
+    last_opp()
     attn_grad(1)
 
     def gw_copy(tile):
         cols = pl.ds(pl.multiple_of(tile * TILE, TILE), TILE)
         return pltpu.make_async_copy(gw_v.at[:, cols], gw.at[:, cols], gw_sem.at[tile])
 
-    def weight_grad(half):
-        @pl.loop(4 * half, 4 * half + 4)
+    def weight_grad(first_tile, stop):
+        @pl.loop(first_tile, stop)
         def _(tile):
             cols = pl.ds(pl.multiple_of(tile * TILE, TILE), TILE)
             gw_v[:, cols] = dot(bat_v[...], g_v[:, cols]).astype(BF16)
             gw_copy(tile).start()
 
-    weight_grad(0)
+    weight_grad(0, 4)
 
     landed(rel_l, sl_r.at[0])
     landed(recvp.at[RIGHT, :, half_a], pp_r.at[RIGHT, 0])
@@ -383,7 +407,7 @@
     send_acc_r.start()
     send_acc_l.start()
 
-    weight_grad(1)
+    weight_grad(4, D // TILE)
 
     @pl.loop(0, 4)
     def _(h):
@@ -428,7 +452,7 @@
     resid_copy.wait_send()
     for h in range(4):
         attn_copy(h).wait_send()
-    for copy in (early_to_r, early_to_l, early_z_l, early_z_r):
+    for copy in (early_to_r, early_to_l, onward_r, onward_l, early_z_l, early_z_r, early_z_o):
         copy.wait_send()
     for p in range(len(PIECES)):
         for copy in (z_copy(p), *x_copies(p, p < LAST), *left_copies(p), *right_copies(p)):
@@ -467,6 +491,7 @@
     dma = pltpu.SemaphoreType.DMA
     vmem = pltpu.VMEM
     scratch = [
+        pltpu.SMEM((4, 4), jnp.int32),
         vmem((R, R), BF16), vmem((2, R, HD), BF16), vmem((R, R), BF16), vmem((2, R, HD), BF16),
         vmem((R, D), BF16), vmem((R, D), BF16),
         vmem((4, HD, R), BF16), vmem((4, HD, R), BF16), vmem((64, D), BF16),
@@ -477,8 +502,9 @@
         vmem((4, 2, 64, D), BF16), vmem((4, 64, D), BF16), vmem((2, 64, HALF), BF16), vmem((2, 64, HALF), BF16),
         vmem((64, HALF), BF16), vmem((64, HALF), BF16), vmem((2, 64, HALF), BF16), vmem((2, 64, HALF), BF16),
         vmem((64, HALF), BF16), vmem((64, HALF), BF16), vmem((64, D), BF16),
-        dma((5,)), dma((4,)), dma((D // TILE,)),
-        vmem((CROWS, D), BF16), vmem((CROWS, D), BF16), dma, dma, dma, dma, dma((2,)), dma((2,)),
+        dma((6,)), dma((4,)), dma((D // TILE,)),
+        vmem((CROWS, D), BF16), vmem((CROWS, D), BF16), vmem((CROWS, D), BF16),
+        dma, dma, dma, dma, dma((2,)), dma((2,)), dma((3,)), dma((3,)),
         dma((len(PIECES),)), dma((len(PIECES),)), dma, dma, dma((4,)), dma((4,)), dma, dma,
         dma((LAST,)), dma((LAST,)), dma((LAST,)), dma((LAST,)),
         dma((CHUNKS,)), dma((CHUNKS,)), dma((CHUNKS,)), dma((CHUNKS,)),
@@ -493,7 +519,7 @@
             jax.ShapeDtypeStruct((2, R, HD), BF16),
             jax.ShapeDtypeStruct((R, D), BF16),
         ),
-        in_specs=[smem] * 3 + [pl.BlockSpec(memory_space=pltpu.HBM)] * 7,
+        in_specs=[smem] * 2 + [pl.BlockSpec(memory_space=pltpu.HBM)] * 8,
         out_specs=(any_space,) * 4,
         scratch_shapes=scratch,
         compiler_params=pltpu.CompilerParams(

time: 56.5 us -> 55.2 us (0.977)
  Pallas kernels: 54.4 us -> 53.2 us
    pallas_call x1, Pallas kernels: 51.7 us -> 50.5 us  [shards(): pl.pallas_call(kernel, out_shape=(jax.ShapeDtypeStruct((64, D), BF16), ja...]
where the time goes in v4:
time: 55.2 us; the launch traced here: 55.1 us
  Pallas kernels  53.2 us (96%)
  between operations  1.93 us (3%)
    pallas_call x1, Pallas kernels, shards(): pl.pallas_call(kernel, out_shape=(jax.ShapeDtypeStruct((64, D), BF16), ja...  50.5 us
    pallas_call x1, Pallas kernels, shards(): pl.pallas_call(deliver, out_shape=tuple((jax.ShapeDtypeStruct(a.shape, a....  2.7 us

profile of v4, /device:TPU:1, one launch (start us, length us, event | category | flops | bytes accessed | tf_op | source)
XLA Modules:
  0.0 55.1 jit_solution(4931359003876597024)
XLA Ops:
  1.9 50.5 %shard_map.129 = (bf16[64,4096]{1,0:T(8,128)(2,1)S(1)}, bf16[512,512]{1,0:T(8,128)(2,1)S(1)}, bf16[2,512,128]{2,1,0:T(8,128)(2,1)S(1)}, bf16[512,4096]{1,0:T(8,128)(2,1)S(1)}) custom-call(s32[1]{0:T(128)S(6)} %copy.14.fwd_micro, s32[1]{0:T(128)S(6)} %copy.15.grad_micro, s32[4,4]{1,0:T(4,128)} %starts_h.1, bf16[64,4096]{1,0:T(8,128)(2,1)} %bitcast.15, ...), custom_call_target="tpu_custom_call" | custom-call | tf_op jit(solution)/shard_map/pallas_call | solution.py:514
  52.4 2.7 %shard_map.130 = (bf16[1,512,4096]{2,1,0:T(8,128)(2,1)}, bf16[1,512,512]{2,1,0:T(8,128)(2,1)}, bf16[2,512,128]{2,1,0:T(8,128)(2,1)}, bf16[1,64,4096]{2,1,0:T(8,128)(2,1)}) custom-call(bf16[1,512,4096]{2,1,0:T(8,128)(2,1)S(1)} %bitcast.11, bf16[1,512,512]{2,1,0:T(8,128)(2,1)S(1)} %bitcast.13, bf16[2,512,128]{2,1,0:T(8,128)(2,1)S(1)} %get-tuple-element.14.refs_2_, ...), custom_call_target="tpu_custom_call" | custom-call | tf_op jit(solution)/shard_map/pallas_call | solution.py:537

commit v5 on v4

--- a/solution.py
+++ b/solution.py
@@ -37,10 +37,10 @@
 
 def kernel(
     fwd_micro, grad_micro, starts_h, resid, fq, fkv, bq, bkv, grad, weight,
-    out, gq, gkv, gw,
+    base, gq, gkv, gw, fin_l, fin_r,
     starts, fq_v, fkv_v, bq_v, bkv_v, w_v, g_v, attn_out, attn_in, resid_in, mic_out, mic_in,
     bias_b, kt_v, vt_v, pt_v, bat_v, acc_v, ga_v, dk_v, dv_v, gq_v, gkv_v, gw_v,
-    part, recvp, opp_sum, side_sum, rel_l, rel_r, fin_l, fin_r, acc_r, acc_l, out_v,
+    part, recvp, opp_sum, side_sum, rel_l, rel_r, acc_r, acc_l, base_v,
     ld_sem, st_sem, gw_sem,
     early_l, early_r, early_o, el_s, el_r, er_s, er_r, eo_s, eo_r, ez_s, ez_r,
     z_s, z_r, mic_s, mic_r, at_s, at_r, rs_s, rs_r,
@@ -434,19 +434,18 @@
     resid_copy.wait_recv()
     for half in range(2):
         landed(recvp.at[OWN, :, halves[half]], pp_r.at[OWN, half])
+
+        @pl.loop(0, HALF, step=TILE)
+        def _(cols):
+            place = pl.ds(pl.multiple_of(half * HALF + cols, TILE), TILE)
+            base_v[:, place] = resid_in[:, place].astype(F32) + chip_sum(OWN, half, cols)
+
+    store = pltpu.make_async_copy(base_v, base, st_sem.at[2])
+    store.start()
+    stores.append(store)
+    for half in range(2):
         landed(fin_l.at[half], sl_r.at[2 if half == 0 else 1])
         landed(fin_r.at[half], sr_r.at[1 if half == 0 else 2])
-
-        @pl.loop(0, HALF, step=TILE)
-        def _(cols):
-            window = pl.ds(pl.multiple_of(cols, TILE), TILE)
-            place = pl.ds(pl.multiple_of(half * HALF + cols, TILE), TILE)
-            total = chip_sum(OWN, half, cols) + fin_l[half, :, window].astype(F32) + fin_r[half, :, window].astype(F32)
-            out_v[:, place] = (resid_in[:, place].astype(F32) + total).astype(BF16)
-
-        store = pltpu.make_async_copy(out_v.at[:, halves[half]], out.at[:, halves[half]], st_sem.at[2 + half])
-        store.start()
-        stores.append(store)
 
     mic.wait_send()
     resid_copy.wait_send()
@@ -470,17 +469,36 @@
         store.wait()
 
 
-def deliver(*refs):
-    srcs, dsts, sem = refs[:4], refs[4:8], refs[8]
+def deliver(
+    gw, gq, gkv, base, fin_l, fin_r, gw_out, gq_out, gkv_out, out,
+    base_v, left_v, right_v, out_v, sem, in_sem, out_sem,
+):
+    sides = [
+        pltpu.make_async_copy(src, dst, in_sem.at[i])
+        for i, (src, dst) in enumerate([(base, base_v), (fin_l, left_v), (fin_r, right_v)])
+    ]
     pieces = []
-    for src, dst in zip(srcs, dsts):
-        rows = src.shape[-2]
+    for src, dst in ((gw, gw_out), (gq, gq_out), (gkv, gkv_out)):
         for lead in range(src.shape[0]):
-            for row in range(0, rows, 64):
+            for row in range(0, src.shape[1], 64):
                 pieces.append(tuple(ref.at[lead, pl.ds(row, 64), :] for ref in (src, dst)))
     copies = [pltpu.make_async_copy(a, b, sem.at[i]) for i, (a, b) in enumerate(pieces)]
-    for copy in copies:
+    for copy in (*sides, *copies):
         copy.start()
+    for side in sides:
+        side.wait()
+    for half in range(2):
+
+        @pl.loop(0, HALF, step=TILE)
+        def _(cols):
+            window = pl.ds(pl.multiple_of(cols, TILE), TILE)
+            place = pl.ds(pl.multiple_of(half * HALF + cols, TILE), TILE)
+            total = base_v[:, place] + left_v[half, :, window].astype(F32) + right_v[half, :, window].astype(F32)
+            out_v[:, place] = total.astype(BF16)
+
+        columns = pl.ds(half * HALF, HALF)
+        copies.append(pltpu.make_async_copy(out_v.at[:, columns], out.at[0, :, columns], out_sem.at[half]))
+        copies[-1].start()
     for copy in copies:
         copy.wait()
 
@@ -500,8 +518,8 @@
         vmem((4, R, R), BF16), vmem((R, R), BF16), vmem((R // 2, R), F32), vmem((R, R), BF16),
         vmem((R, HD), F32), vmem((R, HD), F32), vmem((R, R), BF16), vmem((2, R, HD), BF16), vmem((R, D), BF16),
         vmem((4, 2, 64, D), BF16), vmem((4, 64, D), BF16), vmem((2, 64, HALF), BF16), vmem((2, 64, HALF), BF16),
-        vmem((64, HALF), BF16), vmem((64, HALF), BF16), vmem((2, 64, HALF), BF16), vmem((2, 64, HALF), BF16),
-        vmem((64, HALF), BF16), vmem((64, HALF), BF16), vmem((64, D), BF16),
+        vmem((64, HALF), BF16), vmem((64, HALF), BF16),
+        vmem((64, HALF), BF16), vmem((64, HALF), BF16), vmem((64, D), F32),
         dma((6,)), dma((4,)), dma((D // TILE,)),
         vmem((CROWS, D), BF16), vmem((CROWS, D), BF16), vmem((CROWS, D), BF16),
         dma, dma, dma, dma, dma((2,)), dma((2,)), dma((3,)), dma((3,)),
@@ -511,16 +529,18 @@
         dma((4, len(PIECES))), dma((4, len(PIECES))),
         dma((4, 2)), dma((4, 2)), dma((3,)), dma((3,)), dma((3,)), dma((3,)),
     ]
-    out, gq, gkv, gw = pl.pallas_call(
+    base, gq, gkv, gw, fin_l, fin_r = pl.pallas_call(
         kernel,
         out_shape=(
-            jax.ShapeDtypeStruct((64, D), BF16),
+            jax.ShapeDtypeStruct((64, D), F32),
             jax.ShapeDtypeStruct((R, R), BF16),
             jax.ShapeDtypeStruct((2, R, HD), BF16),
             jax.ShapeDtypeStruct((R, D), BF16),
+            jax.ShapeDtypeStruct((2, 64, HALF), BF16),
+            jax.ShapeDtypeStruct((2, 64, HALF), BF16),
         ),
         in_specs=[smem] * 2 + [pl.BlockSpec(memory_space=pltpu.HBM)] * 8,
-        out_specs=(any_space,) * 4,
+        out_specs=(any_space,) * 6,
         scratch_shapes=scratch,
         compiler_params=pltpu.CompilerParams(
             collective_id=0, has_side_effects=True, vmem_limit_bytes=40 * 1024 * 1024
@@ -532,16 +552,22 @@
             for a in (fwd_resid, fwd_query, fwd_keyval, bwd_query, bwd_keyval, grad_in, out_weight)
         ),
     )
-    arrays = (gw[None], gq[None], gkv, out[None])
-    count = sum(a.shape[0] * max(a.shape[1] // 64, 1) for a in arrays)
+    arrays = (gw[None], gq[None], gkv)
+    count = sum(a.shape[0] * (a.shape[1] // 64) for a in arrays)
     gw, gq, gkv, out = pl.pallas_call(
         deliver,
-        out_shape=tuple(jax.ShapeDtypeStruct(a.shape, a.dtype) for a in arrays),
-        in_specs=[any_space] * 4,
+        out_shape=(
+            *(jax.ShapeDtypeStruct(a.shape, a.dtype) for a in arrays),
+            jax.ShapeDtypeStruct((1, 64, D), BF16),
+        ),
+        in_specs=[any_space] * 6,
         out_specs=(any_space,) * 4,
-        scratch_shapes=[dma((count,))],
-        compiler_params=pltpu.CompilerParams(vmem_limit_bytes=4 * 1024 * 1024),
-    )(*arrays)
+        scratch_shapes=[
+            vmem((64, D), F32), vmem((2, 64, HALF), BF16), vmem((2, 64, HALF), BF16), vmem((64, D), BF16),
+            dma((count,)), dma((3,)), dma((2,)),
+        ],
+        compiler_params=pltpu.CompilerParams(vmem_limit_bytes=8 * 1024 * 1024),
+    )(*arrays, base, fin_l, fin_r)
     return (out, gq, gkv[None], gw)
 
 

time: 55.2 us -> 55 us (level)
  no operation moved by 1% of the time
where the time goes in v5:
time: 55 us; the launch traced here: 54.9 us
  Pallas kernels  53 us (96%)
  between operations  1.93 us (4%)
    pallas_call x1, Pallas kernels, shards(): pl.pallas_call(kernel, out_shape=(jax.ShapeDtypeStruct((64, D), F32), jax...  50.1 us
    pallas_call x1, Pallas kernels, shards(): pl.pallas_call(deliver, out_shape=(*(jax.ShapeDtypeStruct(a.shape, a.dtyp...  2.86 us

profile of v5, /device:TPU:1, one launch (start us, length us, event | category | flops | bytes accessed | tf_op | source)
XLA Modules:
  0.0 54.9 jit_solution(10196191394282180219)
XLA Ops:
  1.9 50.1 %shard_map.129 = (f32[64,4096]{1,0:T(8,128)S(1)}, bf16[512,512]{1,0:T(8,128)(2,1)S(1)}, bf16[2,512,128]{2,1,0:T(8,128)(2,1)S(1)}, bf16[512,4096]{1,0:T(8,128)(2,...) custom-call(s32[1]{0:T(128)S(6)} %copy.14.fwd_micro, s32[1]{0:T(128)S(6)} %copy.15.grad_micro, ...), custom_call_target="tpu_custom_call" | custom-call | tf_op jit(solution)/shard_map/pallas_call | solution.py:532
  52.0 2.9 %shard_map.130 = (bf16[1,512,4096]{2,1,0:T(8,128)(2,1)}, bf16[1,512,512]{2,1,0:T(8,128)(2,1)}, bf16[2,512,128]{2,1,0:T(8,128)(2,1)}, bf16[1,64,4096]{2,1,0:T(8,128)(2,1)}) custom-call(bf16[1,512,4096]{2,1,0:T(8,128)(2,1)S(1)} %bitcast.10, bf16[1,512,512]{2,1,0:T(8,128)(2,1)S(1)} %bitcast.11, bf16[2,512,128]{2,1,0:T(8,128)(2,1)S(1)} %get-tuple-element.16.gkv, ...), custom_call_target="tpu_custom_call" | custom-call | tf_op jit(solution)/shard_map/pallas_call | solution.py:557

commit v6 on v5

--- a/solution.py
+++ b/solution.py
@@ -391,23 +391,22 @@
             gw_v[:, cols] = dot(bat_v[...], g_v[:, cols]).astype(BF16)
             gw_copy(tile).start()
 
-    weight_grad(0, 4)
-
-    landed(rel_l, sl_r.at[0])
-    landed(recvp.at[RIGHT, :, half_a], pp_r.at[RIGHT, 0])
-    landed(rel_r, sr_r.at[0])
-    landed(recvp.at[LEFT, :, half_b], pp_r.at[LEFT, 1])
-
-    @pl.loop(0, HALF, step=TILE)
-    def _(cols):
-        window = pl.ds(pl.multiple_of(cols, TILE), TILE)
-        acc_r[:, window] = (chip_sum(RIGHT, 0, cols) + rel_l[:, window].astype(F32)).astype(BF16)
-        acc_l[:, window] = (chip_sum(LEFT, 1, cols) + rel_r[:, window].astype(F32)).astype(BF16)
-
+    weight_grad(0, 3)
+
+    def running_sum(slot, half, arrived, arrival, result):
+        landed(arrived, arrival)
+        landed(recvp.at[slot, :, halves[half]], pp_r.at[slot, half])
+
+        @pl.loop(0, HALF, step=TILE)
+        def _(cols):
+            window = pl.ds(pl.multiple_of(cols, TILE), TILE)
+            result[:, window] = (chip_sum(slot, half, cols) + arrived[:, window].astype(F32)).astype(BF16)
+
+    running_sum(RIGHT, 0, rel_l, sl_r.at[0], acc_r)
     send_acc_r.start()
+    running_sum(LEFT, 1, rel_r, sr_r.at[0], acc_l)
     send_acc_l.start()
-
-    weight_grad(4, D // TILE)
+    weight_grad(3, D // TILE)
 
     @pl.loop(0, 4)
     def _(h):
@@ -480,8 +479,9 @@
     pieces = []
     for src, dst in ((gw, gw_out), (gq, gq_out), (gkv, gkv_out)):
         for lead in range(src.shape[0]):
-            for row in range(0, src.shape[1], 64):
-                pieces.append(tuple(ref.at[lead, pl.ds(row, 64), :] for ref in (src, dst)))
+            step = 64 if src.shape[2] == D else src.shape[1]
+            for row in range(0, src.shape[1], step):
+                pieces.append(tuple(ref.at[lead, pl.ds(row, step), :] for ref in (src, dst)))
     copies = [pltpu.make_async_copy(a, b, sem.at[i]) for i, (a, b) in enumerate(pieces)]
     for copy in (*sides, *copies):
         copy.start()
@@ -553,7 +553,7 @@
         ),
     )
     arrays = (gw[None], gq[None], gkv)
-    count = sum(a.shape[0] * (a.shape[1] // 64) for a in arrays)
+    count = R // 64 + 1 + 2
     gw, gq, gkv, out = pl.pallas_call(
         deliver,
         out_shape=(

time: 55 us -> 54.2 us (0.985)
  Pallas kernels: 53 us -> 52.2 us
    pallas_call x1, Pallas kernels: 50.1 us -> 49.5 us  [shards(): pl.pallas_call(kernel, out_shape=(jax.ShapeDtypeStruct((64, D), F32), jax...]
where the time goes in v6:
time: 54.2 us; the launch traced here: 54.1 us
  Pallas kernels  52.2 us (96%)
  between operations  1.93 us (4%)
    pallas_call x1, Pallas kernels, shards(): pl.pallas_call(kernel, out_shape=(jax.ShapeDtypeStruct((64, D), F32), jax...  49.5 us
    pallas_call x1, Pallas kernels, shards(): pl.pallas_call(deliver, out_shape=(*(jax.ShapeDtypeStruct(a.shape, a.dtyp...  2.68 us

profile of v6, /device:TPU:1, one launch (start us, length us, event | category | flops | bytes accessed | tf_op | source)
XLA Modules:
  0.0 54.1 jit_solution(4753772175835126729)
XLA Ops:
  1.9 49.5 %shard_map.129 = (f32[64,4096]{1,0:T(8,128)S(1)}, bf16[512,512]{1,0:T(8,128)(2,1)S(1)}, bf16[2,512,128]{2,1,0:T(8,128)(2,1)S(1)}, bf16[512,4096]{1,0:T(8,128)(2,...) custom-call(s32[1]{0:T(128)S(6)} %copy.14.fwd_micro, s32[1]{0:T(128)S(6)} %copy.15.grad_micro, ...), custom_call_target="tpu_custom_call" | custom-call | tf_op jit(solution)/shard_map/pallas_call | solution.py:532
  51.4 2.7 %shard_map.130 = (bf16[1,512,4096]{2,1,0:T(8,128)(2,1)}, bf16[1,512,512]{2,1,0:T(8,128)(2,1)}, bf16[2,512,128]{2,1,0:T(8,128)(2,1)}, bf16[1,64,4096]{2,1,0:T(8,128)(2,1)}) custom-call(bf16[1,512,4096]{2,1,0:T(8,128)(2,1)S(1)} %bitcast.10, bf16[1,512,512]{2,1,0:T(8,128)(2,1)S(1)} %bitcast.11, bf16[2,512,128]{2,1,0:T(8,128)(2,1)S(1)} %get-tuple-element.16.gkv, ...), custom_call_target="tpu_custom_call" | custom-call | tf_op jit(solution)/shard_map/pallas_call | solution.py:557
